TPU v7x, 32 devices: a whole 2x2x4 slice. The times are simulated.
32 devices in a mesh: conv: 4 (over y, core), seq: 4 (over z), tensor: 2 (over x).
Axes of the slice: x: 2, y: 2, z: 4, core: 2. Of those that a mesh axis runs over, the one named last changes fastest.
Arguments:
- queries: bfloat16 [4, 512, 4096], P('conv', 'seq', 'tensor'), may hold values from -6 to 6
- keys: bfloat16 [8, 1664, 1024], P('conv', ('seq', 'tensor')), may hold values from -6 to 6
- values: bfloat16 [8, 1664, 1024], P('conv', ('seq', 'tensor')), may hold values from -18 to 18
- q_gain: float32 [128], replicated, may hold values from 0.9 to 2.2
- k_gain: float32 [128], replicated, may hold values from 0.9 to 2.2
- gate: float32 [1], replicated, may hold values from 0.4 to 1.6
- tile_count: int32 [4], replicated, may hold values from 1 to 2, as said below
- tile_owner: int32 [4, 2], replicated, may hold values from -1 to 3, as said below
- visible: int32 [4, 512], replicated, may hold values from 0 to 2, as said below
- d_out: bfloat16 [4, 512, 4096], P('conv', 'seq', 'tensor'), may hold values from -12 to 12
Outputs:
- attended: bfloat16 [4, 512, 4096], P('conv', 'seq', 'tensor')
- d_queries: bfloat16 [4, 512, 4096], P('conv', 'seq', 'tensor')
- d_keys: bfloat16 [8, 1664, 1024], P('conv', ('seq', 'tensor'))
- d_values: bfloat16 [8, 1664, 1024], P('conv', ('seq', 'tensor'))
Inputs may be any that keep to these rules, and one draw needn't show every extreme that they name: `tile_count`: some conversation has 2 tiles. `tile_owner`: entries with t at or past the conversation's count are -1. The tiles of one conversation have different owners, no two tiles share a slot, and some conv index holds 2 tiles. `visible`: never falls along a conversation's text; it is 0 at the first token and 2 at the last.
All inputs are finite; a program needn't handle non-finite values.
Results may differ from a plain program's by a relative error of at most 0.02.
Values may be sent and summed in bfloat16 or wider, within the bound.
A program may use at most 128 MiB of HBM per device.

v0:
```python
from functools import partial
import math

import jax
import jax.numpy as jnp
from jax import lax
from jax.sharding import PartitionSpec as P

TILE = 1601


EPSILON = 1e-05


def head_norm(inputs, norm_gain):
    mean_square = jnp.mean(inputs * inputs, axis=-1, keepdims=True)
    return inputs * lax.rsqrt(mean_square + EPSILON) * norm_gain


def key_mask(seen_tiles, tile_index, row_start, row_count):
    row_ids = row_start + jnp.arange(row_count, dtype=jnp.int32)
    return (seen_tiles > tile_index)[:, None] & (row_ids < TILE)[None, :]


def tile_weights(query_bf, key_tile, visible_keys, score_scale):
    scores = (
        jnp.einsum("pkgd,rkd->kgpr", query_bf, key_tile, preferred_element_type=jnp.float32)
        * score_scale
    )
    return jnp.where(visible_keys[None, None], jnp.exp(scores), 0.0)


def tile_forward(query_bf, key_tile, value_tile, visible_keys, score_scale):
    weights = tile_weights(query_bf, key_tile, visible_keys, score_scale)
    weighted = jnp.einsum(
        "kgpr,rkd->pkgd",
        weights.astype(jnp.bfloat16),
        value_tile,
        preferred_element_type=jnp.float32,
    )
    return (jnp.sum(weights, axis=-1), weighted)


def tile_gradients(
    query_bf,
    grad_bf,
    key_tile,
    value_tile,
    visible_keys,
    safe_sum,
    row_delta,
    score_scale,
    block_count,
):
    weights = tile_weights(query_bf, key_tile, visible_keys, score_scale)
    probability = weights / safe_sum[..., None]
    grad_prob = jnp.einsum(
        "pkgd,rkd->kgpr", grad_bf, value_tile, preferred_element_type=jnp.float32
    )
    grad_score = (probability * (grad_prob - row_delta[..., None])).astype(jnp.bfloat16)
    prob_bf = probability.astype(jnp.bfloat16)
    grad_query = (
        jnp.einsum("kgpr,rkd->pkgd", grad_score, key_tile, preferred_element_type=jnp.float32)
        * score_scale
    )
    kv_local, group_size, token_count, row_count = grad_score.shape
    head_size = query_bf.shape[-1]
    block_tokens = token_count // block_count
    score_blocks = grad_score.reshape(kv_local, group_size, block_count, block_tokens, row_count)
    prob_blocks = prob_bf.reshape(kv_local, group_size, block_count, block_tokens, row_count)
    query_blocks = query_bf.reshape(block_count, block_tokens, kv_local, group_size, head_size)
    grad_blocks = grad_bf.reshape(block_count, block_tokens, kv_local, group_size, head_size)
    key_part = (
        jnp.einsum(
            "kgbpr,bpkgd->brkd", score_blocks, query_blocks, preferred_element_type=jnp.float32
        )
        * score_scale
    )
    value_part = jnp.einsum(
        "kgbpr,bpkgd->brkd", prob_blocks, grad_blocks, preferred_element_type=jnp.float32
    )
    key_part = jnp.sum(
        lax.optimization_barrier(key_part.astype(jnp.bfloat16)).astype(jnp.float32), axis=0
    )
    value_part = jnp.sum(
        lax.optimization_barrier(value_part.astype(jnp.bfloat16)).astype(jnp.float32), axis=0
    )
    return (
        grad_query,
        key_part.reshape(row_count, kv_local * head_size),
        value_part.reshape(row_count, kv_local * head_size),
    )


def attend_forward(query_bf, tile_keys, tile_values, seen_tiles, row_start, score_scale):
    row_count, slot_count, features = tile_keys.shape
    token_count, kv_local, group_size, head_size = query_bf.shape
    weight_sum = jnp.zeros((kv_local, group_size, token_count), jnp.float32)
    weighted = jnp.zeros(query_bf.shape, jnp.float32)
    for tile_index in range(slot_count):
        key_tile = tile_keys[:, tile_index].reshape(row_count, kv_local, head_size)
        value_tile = tile_values[:, tile_index].reshape(row_count, kv_local, head_size)
        visible_keys = key_mask(seen_tiles, tile_index, row_start, row_count)
        work = partial(tile_forward, query_bf, key_tile, value_tile, visible_keys, score_scale)
        part_sum, part_weighted = work()
        weight_sum = weight_sum + part_sum
        weighted = weighted + part_weighted
    return (weight_sum, weighted)


def attend_backward(
    query_bf,
    grad_bf,
    tile_keys,
    tile_values,
    seen_tiles,
    row_start,
    safe_sum,
    row_delta,
    score_scale,
    block_tokens,
):
    row_count, slot_count, features = tile_keys.shape
    token_count, kv_local, group_size, head_size = query_bf.shape
    block_count = token_count // block_tokens
    grad_query = jnp.zeros(query_bf.shape, jnp.float32)
    key_parts = []
    value_parts = []
    for tile_index in range(slot_count):
        key_tile = tile_keys[:, tile_index].reshape(row_count, kv_local, head_size)
        value_tile = tile_values[:, tile_index].reshape(row_count, kv_local, head_size)
        visible_keys = key_mask(seen_tiles, tile_index, row_start, row_count)
        work = partial(
            tile_gradients,
            query_bf,
            grad_bf,
            key_tile,
            value_tile,
            visible_keys,
            safe_sum,
            row_delta,
            score_scale,
            block_count,
        )
        part_query, key_part, value_part = work()
        grad_query = grad_query + part_query
        key_parts.append(key_part)
        value_parts.append(value_part)
    return (grad_query, jnp.stack(key_parts, axis=1), jnp.stack(value_parts, axis=1))


def shards(queries, keys, values, q_gain, k_gain, gate, tile_count, tile_owner, visible, d_out):
    conv_count = lax.axis_size("conv")
    tensor_count = lax.axis_size("tensor")
    conv_index = lax.axis_index("conv")
    sequence_index = lax.axis_index("seq")
    slot_count, row_local, features = keys.shape
    head_size = q_gain.shape[0]
    kv_heads = features // head_size
    kv_local = kv_heads // tensor_count
    token_count = queries.shape[1]
    query_heads = queries.shape[2] // head_size
    group_size = query_heads // kv_local
    score_scale = 1.0 / math.sqrt(head_size)
    gate_value = jnp.tanh(gate[0])
    conv_ids = jnp.arange(conv_count, dtype=jnp.int32)
    transfers = (tile_owner == conv_index).astype(jnp.bfloat16)
    own_owners = lax.dynamic_index_in_dim(tile_owner, conv_index, 0, keepdims=False)
    takes = (own_owners[:, None] == conv_ids[None, :]).astype(jnp.bfloat16)
    own_count = lax.dynamic_index_in_dim(tile_count, conv_index, 0, keepdims=False)
    seen_all = jnp.minimum(
        lax.dynamic_index_in_dim(visible, conv_index, 0, keepdims=False), own_count
    )
    key_raw = keys.astype(jnp.float32).reshape(slot_count, row_local, kv_heads, head_size)
    key_normed, key_back = jax.vjp(lambda inputs: head_norm(inputs, k_gain), key_raw)
    key_halfprec = key_normed.astype(jnp.bfloat16).reshape(slot_count, row_local, features)
    outgoing_keys = jnp.einsum(
        "wn,nki->wki", transfers, key_halfprec, preferred_element_type=jnp.float32
    ).astype(jnp.bfloat16)
    send_values = jnp.einsum(
        "wn,nki->wki", transfers, values, preferred_element_type=jnp.float32
    ).astype(jnp.bfloat16)
    got_keys, got_values = (
        lax.all_to_all(
            lax.all_to_all(outgoing_keys, "conv", split_axis=0, concat_axis=0, tiled=True),
            "tensor",
            split_axis=2,
            concat_axis=1,
            tiled=True,
        ),
        lax.all_to_all(
            lax.all_to_all(send_values, "conv", split_axis=0, concat_axis=0, tiled=True),
            "tensor",
            split_axis=2,
            concat_axis=1,
            tiled=True,
        ),
    )
    tile_keys = jnp.einsum(
        "to,orf->rtf", takes, got_keys, preferred_element_type=jnp.float32
    ).astype(jnp.bfloat16)
    tile_values = jnp.einsum(
        "to,orf->rtf", takes, got_values, preferred_element_type=jnp.float32
    ).astype(jnp.bfloat16)
    query_raw = queries[0].astype(jnp.float32).reshape(token_count, query_heads, head_size)
    query_normed, query_back = jax.vjp(lambda inputs: head_norm(inputs, q_gain), query_raw)
    query_bf = query_normed.astype(jnp.bfloat16).reshape(
        token_count, kv_local, group_size, head_size
    )
    grad_bf = (
        (gate_value * d_out[0].astype(jnp.float32))
        .astype(jnp.bfloat16)
        .reshape(token_count, kv_local, group_size, head_size)
    )
    own_start = sequence_index * token_count
    all_queries = lax.all_gather(query_bf, "seq", axis=0, tiled=True)
    all_grads = lax.all_gather(grad_bf, "seq", axis=0, tiled=True)
    share_rows = tile_keys.shape[0]
    row_start = sequence_index * share_rows
    part_sum, part_weighted = attend_forward(
        all_queries, tile_keys, tile_values, seen_all, row_start, score_scale
    )
    all_weighted, all_weight_sum = (
        lax.psum(part_weighted.astype(jnp.bfloat16), "seq").astype(jnp.float32),
        lax.psum(part_sum.astype(jnp.bfloat16), "seq").astype(jnp.float32),
    )
    safe_all = jnp.where(all_weight_sum > 0, all_weight_sum, 1.0)
    context_all = all_weighted / jnp.transpose(safe_all, (2, 0, 1))[..., None]
    context = lax.dynamic_slice_in_dim(context_all, own_start, token_count, 0)
    row_delta = jnp.transpose(
        jnp.sum(all_grads.astype(jnp.float32) * context_all, axis=-1), (1, 2, 0)
    )
    grad_part, key_sums, value_sums = attend_backward(
        all_queries,
        all_grads,
        tile_keys,
        tile_values,
        seen_all,
        row_start,
        safe_all,
        row_delta,
        score_scale,
        token_count,
    )
    grad_query = lax.psum_scatter(
        grad_part.astype(jnp.bfloat16), "seq", scatter_dimension=0, tiled=True
    ).astype(jnp.float32)
    attended = (
        (gate_value * context).astype(jnp.bfloat16).reshape(1, token_count, query_heads * head_size)
    )
    key_round = key_sums.astype(jnp.bfloat16)
    value_round = value_sums.astype(jnp.bfloat16)
    back_keys = jnp.einsum(
        "to,rtf->orf", takes, key_round, preferred_element_type=jnp.float32
    ).astype(jnp.bfloat16)
    back_values = jnp.einsum(
        "to,rtf->orf", takes, value_round, preferred_element_type=jnp.float32
    ).astype(jnp.bfloat16)
    returned_keys, returned_values = (
        lax.all_to_all(
            lax.all_to_all(back_keys, "conv", split_axis=0, concat_axis=0, tiled=True),
            "tensor",
            split_axis=1,
            concat_axis=2,
            tiled=True,
        ),
        lax.all_to_all(
            lax.all_to_all(back_values, "conv", split_axis=0, concat_axis=0, tiled=True),
            "tensor",
            split_axis=1,
            concat_axis=2,
            tiled=True,
        ),
    )
    positioned_keys = jnp.einsum(
        "ew,eig->wig", transfers, returned_keys, preferred_element_type=jnp.float32
    )
    d_values = jnp.einsum(
        "ew,eig->wig", transfers, returned_values, preferred_element_type=jnp.float32
    ).astype(jnp.bfloat16)
    d_keys = key_back(positioned_keys.reshape(slot_count, row_local, kv_heads, head_size))[0]
    d_keys = d_keys.astype(jnp.bfloat16).reshape(slot_count, row_local, features)
    d_queries = query_back(grad_query.reshape(token_count, query_heads, head_size))[0]
    d_queries = d_queries.astype(jnp.bfloat16).reshape(1, token_count, query_heads * head_size)
    return (attended, d_queries, d_keys, d_values)


def solution(mesh):
    in_specs = (
        P("conv", "seq", "tensor"),
        P("conv", ("seq", "tensor"), None),
        P("conv", ("seq", "tensor"), None),
        P(),
        P(),
        P(),
        P(),
        P(),
        P(),
        P("conv", "seq", "tensor"),
    )
    out_specs = (
        P("conv", "seq", "tensor"),
        P("conv", "seq", "tensor"),
        P("conv", ("seq", "tensor"), None),
        P("conv", ("seq", "tensor"), None),
    )
    return jax.shard_map(shards, mesh=mesh, in_specs=in_specs, out_specs=out_specs, check_vma=False)
```

profile of v0, /device:TPU:0, one launch (start us, length us, event | category | flops | bytes accessed | tf_op | source)
XLA Modules:
  0.0 426.6 jit_solution(4525607871681992089)
XLA Ops:
  18.6 4.4 %all-to-all-start.2 = ((bf16[4,208,1024]{2,1,0:T(8,128)(2,1)}), bf16[4,208,1024]{2,1,0:T(8,128)(2,1)}, u32[]{:S(2)}, u32[]{:S(2)}) async-start(bf16[4,208,1024]{2,1,0:T(8,128)(2,1)} %copy.195), calls=%async_computation.2 | async-start | bytes 3407872 | tf_op jit(solution)/shard_map/all_to_all | solution.py:185
  29.1 16.1 %all-to-all-done.2 = bf16[4,208,1024]{2,1,0:T(8,128)(2,1)} async-done(((bf16[4,208,1024]{2,1,0:T(8,128)(2,1)}), bf16[4,208,1024]{2,1,0:T(8,128)(2,1)}, u32[]{:S(2)}, u32[]{:S(2)}) %all-to-all-start.2) | async-done | bytes 1703968 | tf_op jit(solution)/shard_map/all_to_all | solution.py:185
  45.1 3.6 all-to-all-start
  48.7 4.2 copy.196
  53.0 17.2 %all-to-all-done = bf16[4,208,1024]{2,1,0:T(8,128)(2,1)S(1)} async-done(((bf16[4,208,1024]{2,1,0:T(8,128)(2,1)}), bf16[4,208,1024]{2,1,0:T(8,128)(2,1)S(1)}, u32[]{:S(2)}, u32[]{:S(2)}) %all-to-all-start) | async-done | bytes 1703968 | tf_op jit(solution)/shard_map/all_to_all | solution.py:192
  71.4 3.8 all-to-all-start.3
  79.2 4.2 copy.190
  83.4 17.2 %all-to-all-done.3 = bf16[4,208,1024]{1,0,2:T(4,128)(2,1)S(1)} async-done(((bf16[4,208,1024]{1,0,2:T(4,128)(2,1)}), bf16[4,208,1024]{1,0,2:T(4,128)(2,1)S(1)}, u32[]{:S(2)}, u32[]{:S(2)}) %all-to-all-start.3) | async-done | bytes 1703968 | tf_op jit(solution)/shard_map/all_to_all | solution.py:184
  100.6 4.8 %all-to-all-start.1 = ((bf16[4,208,1024]{1,0,2:T(4,128)(2,1)}), bf16[4,208,1024]{1,0,2:T(4,128)(2,1)}, u32[]{:S(2)}, u32[]{:S(2)}) async-start(bf16[4,208,1024]{1,0,2:T(4,128)(2,1)} %copy.190), calls=%async_computation.1 | async-start | bytes 4194304 | tf_op jit(solution)/shard_map/all_to_all | solution.py:191
  105.9 3.9 copy.197
  112.4 3.7 slice_reduce_fusion.2
  117.9 12.1 %all-to-all-done.1 = bf16[4,208,1024]{1,0,2:T(4,128)(2,1)} async-done(((bf16[4,208,1024]{1,0,2:T(4,128)(2,1)}), bf16[4,208,1024]{1,0,2:T(4,128)(2,1)}, u32[]{:S(2)}, u32[]{:S(2)}) %all-to-all-start.1) | async-done | bytes 1703968 | tf_op jit(solution)/shard_map/all_to_all | solution.py:191
  129.9 5.4 %copy.191 = bf16[4,208,2,512]{3,0,1,2:T(4,128)(2,1)S(1)} copy(bf16[4,208,2,512]{1,0,3,2:T(4,128)(2,1)} %bitcast.2) | data formatting | bytes 3407872 | tf_op jit(solution)/shard_map/all_to_all | solution.py:191
  136.4 3.7 slice_reduce_fusion.3
  140.4 8.4 %fusion.8 = (f32[4,4,512]{2,1,0:T(4,128)S(1)}, f32[4,416,512,4]{2,1,3,0:T(8,128)}) fusion(pred[512,416]{0,1:T(8,128)(4,1)S(1)} %get-tuple-element.37, bf16[512,4,4,128]{3,0,2,1:T(8,128)(2,1)} %all-gather.3.cloned.1.call-done, bf16[416,4,128,1]{2,1,0,3:T(4,128)(2,1)S(1)} %bitcast.268), kind=kOutput, calls=%fused_computation.12 | convolution fusion | flops 882630656 | bytes 16400384 | tf_op jit(solution)/shard_map/pkgd,rkd->kgpr/dot_general | solution.py:27
  148.8 6.6 %fusion.5 = (f32[4,4,512]{2,1,0:T(4,128)S(1)}, f32[4,416,512,4]{2,1,3,0:T(8,128)}) fusion(pred[512,416]{0,1:T(8,128)(4,1)S(1)} %get-tuple-element.36, bf16[512,4,4,128]{3,0,2,1:T(8,128)(2,1)S(1)} %copy-done.38, bf16[416,4,128,1]{2,1,0,3:T(4,128)(2,1)S(1)} %bitcast.270), kind=kOutput, calls=%fused_computation.9 | convolution fusion | flops 882630656 | bytes 16400384 | tf_op jit(solution)/shard_map/pkgd,rkd->kgpr/dot_general | solution.py:27
  155.5 19.6 %psum.15 = bf16[4,4,512]{2,1,0:T(4,128)(2,1)S(1)} all-reduce(bf16[4,4,512]{2,1,0:T(4,128)(2,1)S(1)} %add_convert_fusion.1), channel_id=1, replica_groups=mesh['conv'=4,'seq'=4,'tensor'=2] {'seq'}, use_global_device_ids=true, to_apply=%region_5.6 | all-reduce | flops 8192 | bytes 32768 | tf_op jit(solution)/shard_map/psum | solution.py:225
  175.0 6.4 %fusion.10 = f32[4,128,4,512]{3,1,2,0:T(8,128)S(1)} fusion(f32[4,416,512,4]{2,1,3,0:T(8,128)} %get-tuple-element.41, pred[512,416]{0,1:T(8,128)(4,1)S(1)} %get-tuple-element.37, bf16[416,4,128,1]{2,1,0,3:T(4,128)(2,1)S(1)} %bitcast.262), kind=kOutput, calls=%fused_computation.14 | convolution fusion | flops 882638848 | bytes 18464768 | tf_op jit(solution)/shard_map/kgpr,rkd->pkgd/dot_general | solution.py:35
  183.8 3.9 fusion.34
  187.7 15.6 %convert_bitcast_fusion.1 = (bf16[4,4,52,4,8,128]{5,4,3,2,1,0:T(8,128)(2,1)}, bf16[4,4,52,4,8,128]{5,4,3,2,1,0:T(8,128)(2,1)}) fusion(f32[4,4,512]{2,1,0:T(4,128)S(1)} %get-tuple-element.34, f32[4,416,512,4]{2,1,3,0:T(8,128)} %get-tuple-element.39, pred[512,416]{0,1:T(8,128)(4,1)S(1)} %get-tuple-element.36, f32[4,416,512,4]{2,1,3,0:T(8,128)} %get-tuple-element.41, ...), kind=kLoop, calls=%fused_computation.29 | loop fusion | flops 27262976 | bytes 41353216
  208.5 6.7 %fusion.62 = bf16[4,416,4,128]{3,1,2,0:T(8,128)(2,1)} fusion(bf16[4,128,4,4,128]{4,1,3,2,0:T(8,128)(2,1)} %copy.227, bf16[4,4,52,4,8,128]{5,4,3,2,1,0:T(8,128)(2,1)} %get-tuple-element.32), kind=kOutput, calls=%fused_computation.69 | convolution fusion | flops 873267200 | bytes 10616832 | tf_op jit(solution)/shard_map/kgbpr,bpkgd->brkd/dot_general | solution.py:79
  215.2 2.7 reduce.2
  219.9 3.6 stack_reshape.22
  223.5 6.1 %fusion.65 = bf16[4,416,4,128]{3,1,2,0:T(8,128)(2,1)} fusion(bf16[4,128,4,4,128]{4,1,3,2,0:T(8,128)(2,1)S(1)} %copy-done.17, bf16[4,4,52,4,8,128]{5,4,3,2,1,0:T(8,128)(2,1)} %get-tuple-element.33), kind=kOutput, calls=%fused_computation.70 | convolution fusion | flops 873267200 | bytes 10616832 | tf_op jit(solution)/shard_map/kgbpr,bpkgd->brkd/dot_general | solution.py:79
  232.7 3.7 convolution_convert_fusion
  238.0 4.4 %all-to-all-start.6 = ((bf16[4,416,512]{2,1,0:T(8,128)(2,1)}), bf16[4,416,512]{2,1,0:T(8,128)(2,1)}, u32[]{:S(2)}, u32[]{:S(2)}) async-start(bf16[4,416,512]{2,1,0:T(8,128)(2,1)} %copy.235), calls=%async_computation.6 | async-start | bytes 3407872 | tf_op jit(solution)/shard_map/all_to_all | solution.py:268
  242.5 28.4 %all-reduce.2.cloned.1.call-done = bf16[512,4,4,128]{0,3,2,1:T(8,128)(2,1)} async-done(((bf16[512,4,4,128]{0,3,2,1:T(8,128)(2,1)}), bf16[512,4,4,128]{0,3,2,1:T(8,128)(2,1)}) %all-reduce.2.cloned.1.call-update) | async-done | bytes 2097168 | tf_op jit(solution)/shard_map/psum | solution.py:224
  270.9 4.5 %multiply_reduce_fusion = (f32[512,4,4]{0,2,1:T(4,128)S(1)}, f32[512,4,4,128]{0,3,2,1:T(8,128)}) fusion(bf16[512,4,4,128]{0,3,2,1:T(8,128)(2,1)S(1)} %copy-done.8, f32[512,4,4]{0,2,1:T(4,128)S(1)} %get-tuple-element.35, bf16[512,4,4,128]{0,3,2,1:T(8,128)(2,1)} %all-reduce.2.cloned.1.call-done), kind=kLoop, calls=%fused_computation.37 | loop fusion | flops 5234688 | bytes 8454144 | tf_op jit(solution)/shard_map/reduce_sum | solution.py:231
  275.4 7.5 %fusion.1 = bf16[4,4,512,416]{2,3,1,0:T(8,128)(2,1)S(1)} fusion(bf16[512,4,4,128]{0,3,2,1:T(8,128)(2,1)S(1)} %copy-done.8, f32[4,4,512]{2,1,0:T(4,128)S(1)} %bitcast.273, f32[4,4,512]{2,1,0:T(4,128)S(1)} %get-tuple-element.34, f32[4,416,512,4]{2,1,3,0:T(8,128)} %get-tuple-element.41, pred[512,416]{0,1:T(8,128)(4,1)S(1)} %get-tuple-element.37, ...), kind=kOutput, calls=%fused_computation.2 | convolution fusion | flops 892862464 | bytes 23248896 | tf_op jit(solution)/shard_map/pkgd,rkd->kgpr/dot_general | solution.py:57
  282.8 2.7 copy-done.9
  285.6 3.2 fusion.57
  293.5 7.3 %fusion.3 = bf16[4,4,512,416]{2,3,1,0:T(8,128)(2,1)S(1)} fusion(bf16[512,4,4,128]{0,3,2,1:T(8,128)(2,1)S(1)} %copy-done.8, f32[4,4,512]{2,1,0:T(4,128)S(1)} %bitcast.274, f32[4,4,512]{2,1,0:T(4,128)S(1)} %get-tuple-element.34, f32[4,416,512,4]{2,1,3,0:T(8,128)} %get-tuple-element.39, pred[512,416]{0,1:T(8,128)(4,1)S(1)} %get-tuple-element.36, ...), kind=kOutput, calls=%fused_computation.5 | convolution fusion | flops 892862464 | bytes 23248896 | tf_op jit(solution)/shard_map/pkgd,rkd->kgpr/dot_general | solution.py:57
  300.9 2.8 copy-done.10
  307.3 4.3 %fusion.86 = f32[4,128,4,512]{3,1,2,0:T(8,128)S(1)} fusion(bf16[4,4,512,416]{2,3,1,0:T(8,128)(2,1)} %copy-done.10, bf16[416,4,128,1]{2,1,0,3:T(4,128)(2,1)S(1)} %bitcast.271), kind=kOutput, calls=%fused_computation.105 | convolution fusion | flops 872415232 | bytes 11436032 | tf_op jit(solution)/shard_map/kgpr,rkd->pkgd/dot_general | solution.py:63
  311.6 4.4 %multiply_convert_fusion = bf16[4,128,4,512]{3,1,2,0:T(8,128)(2,1)S(1)} fusion(f32[4,128,4,512]{3,1,2,0:T(8,128)S(1)} %fusion.86, bf16[4,4,512,416]{2,3,1,0:T(8,128)(2,1)} %copy-done.9, bf16[416,4,128,1]{2,1,0,3:T(4,128)(2,1)S(1)} %bitcast.269), kind=kOutput, calls=%fused_computation.36 | convolution fusion | flops 875560960 | bytes 13533184 | tf_op jit(solution)/shard_map/kgpr,rkd->pkgd/dot_general | solution.py:63
  318.6 4.0 convolution_convert_fusion.1
  324.0 3.6 all-to-all-start.4
  327.6 3.9 copy.236
  331.6 17.5 %all-to-all-done.4 = bf16[4,416,512]{2,1,0:T(8,128)(2,1)S(1)} async-done(((bf16[4,416,512]{2,1,0:T(8,128)(2,1)}), bf16[4,416,512]{2,1,0:T(8,128)(2,1)S(1)}, u32[]{:S(2)}, u32[]{:S(2)}) %all-to-all-start.4) | async-done | bytes 1703968 | tf_op jit(solution)/shard_map/all_to_all | solution.py:261
  350.2 3.7 all-to-all-start.7
  353.9 4.0 copy.220
  357.9 16.7 %all-to-all-done.7 = bf16[4,416,512]{2,0,1:T(4,128)(2,1)S(1)} async-done(((bf16[4,416,512]{2,0,1:T(4,128)(2,1)}), bf16[4,416,512]{2,0,1:T(4,128)(2,1)S(1)}, u32[]{:S(2)}, u32[]{:S(2)}) %all-to-all-start.7) | async-done | bytes 1703968 | tf_op jit(solution)/shard_map/all_to_all | solution.py:267
  375.8 3.7 all-to-all-start.5
  381.9 5.2 %copy.357 = bf16[4,2,208,512]{3,1,0,2:T(2,128)(2,1)} copy(bf16[4,2,208,512]{3,0,2,1:T(4,128)(2,1)} %bitcast.254) | data formatting | bytes 3407872 | tf_op jit(solution)/shard_map/all_to_all | solution.py:267
  387.1 5.7 %all_to_all.83 = bf16[4,208,1024]{2,0,1:T(4,128)(2,1)} reshape(bf16[4,208,2,512]{3,2,0,1:T(2,128)(2,1)} %bitcast.256) | data formatting | bytes 3407872 | tf_op jit(solution)/shard_map/all_to_all | solution.py:267
  396.4 2.9 all-to-all-done.5
  399.3 2.9 copy.358
  402.3 5.1 %all_to_all.78 = bf16[4,208,1024]{2,1,0:T(8,128)(2,1)} reshape(bf16[4,208,2,512]{3,2,1,0:T(2,128)(2,1)} %bitcast.257) | data formatting | bytes 3407872 | tf_op jit(solution)/shard_map/all_to_all | solution.py:260
  (164 shorter events, 74.8 us)
Async XLA Ops:
  7.2 18.6 %copy-start = (bf16[2,208,1024]{2,1,0:T(8,128)(2,1)S(1)}, bf16[2,208,1024]{2,1,0:T(8,128)(2,1)}, u32[]{:S(2)}) copy-start(bf16[2,208,1024]{2,1,0:T(8,128)(2,1)} %param.12) | copy-start | bytes 2555908
  8.6 1.2 copy-start.3
  9.8 5.2 %copy-start.35 = (f32[128]{0:T(128)S(1)}, f32[128]{0:T(128)}, u32[]{:S(2)}) copy-start(f32[128]{0:T(128)} %param.14) | copy-start | bytes 1540
  9.8 5.2 %copy-start.37 = (s32[4,2]{0,1:T(2,128)S(1)}, s32[4,2]{0,1:T(2,128)}, u32[]{:S(2)}) copy-start(s32[4,2]{0,1:T(2,128)} %param.17) | copy-start | bytes 100
  9.8 5.2 %copy-start.16 = (bf16[2,208,1024]{2,1,0:T(8,128)(2,1)S(1)}, bf16[2,208,1024]{2,1,0:T(8,128)(2,1)}, u32[]{:S(2)}) copy-start(bf16[2,208,1024]{2,1,0:T(8,128)(2,1)} %param.11) | copy-start | bytes 2555908
  16.8 6.2 %copy-start.26 = (bf16[1,128,2048]{2,1,0:T(8,128)(2,1)S(1)}, bf16[1,128,2048]{2,1,0:T(8,128)(2,1)}, u32[]{:S(2)}) copy-start(bf16[1,128,2048]{2,1,0:T(8,128)(2,1)} %param.10) | copy-start | bytes 1572868
  18.6 26.6 %all-to-all-start.2 = ((bf16[4,208,1024]{2,1,0:T(8,128)(2,1)}), bf16[4,208,1024]{2,1,0:T(8,128)(2,1)}, u32[]{:S(2)}, u32[]{:S(2)}) async-start(bf16[4,208,1024]{2,1,0:T(8,128)(2,1)} %copy.195), calls=%async_computation.2 | async-start | bytes 3407872 | tf_op jit(solution)/shard_map/all_to_all | solution.py:185
  23.0 1.7 copy-start.34
  23.0 117.4 %all-gather.3.cloned.1.call-start = ((), (), s32[]{:S(2)}) async-start(), calls=%async_computation.9 | async-start | bytes 2621440 | tf_op jit(solution)/shard_map/all_gather | solution.py:216
  23.3 2.5 copy-start.14
  23.4 3.9 copy-start.5
  24.3 3.0 copy-start.30
  45.1 25.0 %all-to-all-start = ((bf16[4,208,1024]{2,1,0:T(8,128)(2,1)}), bf16[4,208,1024]{2,1,0:T(8,128)(2,1)S(1)}, u32[]{:S(2)}, u32[]{:S(2)}) async-start(bf16[4,208,1024]{2,1,0:T(8,128)(2,1)} %copy.189), calls=%async_computation | async-start | bytes 3407872 | tf_op jit(solution)/shard_map/all_to_all | solution.py:192
  48.7 27.1 %copy-start.27 = (bf16[1,128,2048]{2,1,0:T(8,128)(2,1)S(1)}, bf16[1,128,2048]{2,1,0:T(8,128)(2,1)}, u32[]{:S(2)}) copy-start(bf16[1,128,2048]{2,1,0:T(8,128)(2,1)} %param.19) | copy-start | bytes 1572868
  53.0 24.2 %copy-start.41 = (s32[4]{0:T(128)S(1)}, s32[4]{0:T(128)}, u32[]{:S(2)}) copy-start(s32[4]{0:T(128)} %param.16) | copy-start | bytes 52
  70.1 1.2 copy-start.11
  71.4 29.2 %all-to-all-start.3 = ((bf16[4,208,1024]{1,0,2:T(4,128)(2,1)}), bf16[4,208,1024]{1,0,2:T(4,128)(2,1)S(1)}, u32[]{:S(2)}, u32[]{:S(2)}) async-start(bf16[4,208,1024]{1,0,2:T(4,128)(2,1)} %copy.196), calls=%async_computation.3 | async-start | bytes 4194304 | tf_op jit(solution)/shard_map/all_to_all | solution.py:184
  75.1 128.2 %all-gather.5.cloned.1.call-start = ((), (), s32[]{:S(2)}) async-start(), calls=%async_computation.11 | async-start | bytes 2621440 | tf_op jit(solution)/shard_map/all_gather | solution.py:217
  100.6 29.3 %all-to-all-start.1 = ((bf16[4,208,1024]{1,0,2:T(4,128)(2,1)}), bf16[4,208,1024]{1,0,2:T(4,128)(2,1)}, u32[]{:S(2)}, u32[]{:S(2)}) async-start(bf16[4,208,1024]{1,0,2:T(4,128)(2,1)} %copy.190), calls=%async_computation.1 | async-start | bytes 4194304 | tf_op jit(solution)/shard_map/all_to_all | solution.py:191
  105.4 165.5 %all-reduce.2.cloned.1.call-start = ((), (), s32[]{:S(2)}) async-start(), calls=%async_computation.10 | async-start | bytes 4194304 | tf_op jit(solution)/shard_map/psum | solution.py:224
  136.4 3.9 copy-start.20
  140.4 8.4 %copy-start.22 = (bf16[416,4,128]{2,1,0:T(4,128)(2,1)S(1)}, bf16[416,4,128]{2,1,0:T(4,128)(2,1)}, u32[]{:S(2)}) copy-start(bf16[416,4,128]{2,1,0:T(4,128)(2,1)} %reshape_squeeze.17) | copy-start | bytes 1277956
  140.4 8.4 %copy-start.38 = (bf16[512,4,4,128]{3,0,2,1:T(8,128)(2,1)S(1)}, bf16[512,4,4,128]{3,0,2,1:T(8,128)(2,1)}, u32[]{:S(2)}) copy-start(bf16[512,4,4,128]{3,0,2,1:T(8,128)(2,1)} %all-gather.3.cloned.1.call-done) | copy-start | bytes 6291460
  175.0 8.8 %copy-start.2 = (f32[4,416,512,4]{2,1,3,0:T(8,128)S(1)}, f32[4,416,512,4]{2,1,3,0:T(8,128)}, u32[]{:S(2)}) copy-start(f32[4,416,512,4]{2,1,3,0:T(8,128)} %get-tuple-element.39) | copy-start | bytes 40894468
  215.2 8.3 %copy-start.17 = (bf16[4,128,4,4,128]{4,1,3,2,0:T(8,128)(2,1)S(1)}, bf16[4,128,4,4,128]{4,1,3,2,0:T(8,128)(2,1)}, u32[]{:S(2)}) copy-start(bf16[4,128,4,4,128]{4,1,3,2,0:T(8,128)(2,1)} %copy.227) | copy-start | bytes 6291460
  229.6 3.1 copy-start.25
  236.5 34.4 %copy-start.8 = (bf16[512,4,4,128]{0,3,2,1:T(8,128)(2,1)S(1)}, bf16[512,4,4,128]{0,3,2,1:T(8,128)(2,1)}, u32[]{:S(2)}) copy-start(bf16[512,4,4,128]{0,3,2,1:T(8,128)(2,1)} %all-gather.5.cloned.1.call-done) | copy-start | bytes 6291460
  238.0 86.1 %all-to-all-start.6 = ((bf16[4,416,512]{2,1,0:T(8,128)(2,1)}), bf16[4,416,512]{2,1,0:T(8,128)(2,1)}, u32[]{:S(2)}, u32[]{:S(2)}) async-start(bf16[4,416,512]{2,1,0:T(8,128)(2,1)} %copy.235), calls=%async_computation.6 | async-start | bytes 3407872 | tf_op jit(solution)/shard_map/all_to_all | solution.py:268
  242.4 174.0 %reduce-scatter.4.cloned.1.call-start = ((), (), s32[]{:S(2)}) async-start(), calls=%async_computation.12 | async-start | bytes 2621440
  275.4 10.2 %copy-start.39 = (bf16[512,4,4,128]{3,0,2,1:T(8,128)(2,1)S(1)}, bf16[512,4,4,128]{3,0,2,1:T(8,128)(2,1)}, u32[]{:S(2)}) copy-start(bf16[512,4,4,128]{3,0,2,1:T(8,128)(2,1)} %all-gather.3.cloned.1.call-done) | copy-start | bytes 6291460
  282.8 2.7 copy-start.9
  293.5 10.2 %copy-start.40 = (bf16[512,4,4,128]{3,0,2,1:T(8,128)(2,1)S(1)}, bf16[512,4,4,128]{3,0,2,1:T(8,128)(2,1)}, u32[]{:S(2)}) copy-start(bf16[512,4,4,128]{3,0,2,1:T(8,128)(2,1)} %all-gather.3.cloned.1.call-done) | copy-start | bytes 6291460
  300.9 2.8 copy-start.10
  305.6 1.7 copy-start.23
  307.3 4.3 %copy-start.21 = (bf16[416,4,128]{2,1,0:T(4,128)(2,1)S(1)}, bf16[416,4,128]{2,1,0:T(4,128)(2,1)}, u32[]{:S(2)}) copy-start(bf16[416,4,128]{2,1,0:T(4,128)(2,1)} %reshape_squeeze.19) | copy-start | bytes 1277956
  316.1 2.5 copy-start.24
  324.0 25.0 %all-to-all-start.4 = ((bf16[4,416,512]{2,1,0:T(8,128)(2,1)}), bf16[4,416,512]{2,1,0:T(8,128)(2,1)S(1)}, u32[]{:S(2)}, u32[]{:S(2)}) async-start(bf16[4,416,512]{2,1,0:T(8,128)(2,1)} %copy.219), calls=%async_computation.4 | async-start | bytes 3407872 | tf_op jit(solution)/shard_map/all_to_all | solution.py:261
  350.2 24.4 %all-to-all-start.7 = ((bf16[4,416,512]{2,0,1:T(4,128)(2,1)}), bf16[4,416,512]{2,0,1:T(4,128)(2,1)S(1)}, u32[]{:S(2)}, u32[]{:S(2)}) async-start(bf16[4,416,512]{2,0,1:T(4,128)(2,1)} %copy.236), calls=%async_computation.7 | async-start | bytes 3407872 | tf_op jit(solution)/shard_map/all_to_all | solution.py:267
  375.8 23.5 %all-to-all-start.5 = ((bf16[4,416,512]{2,0,1:T(4,128)(2,1)}), bf16[4,416,512]{2,0,1:T(4,128)(2,1)S(1)}, u32[]{:S(2)}, u32[]{:S(2)}) async-start(bf16[4,416,512]{2,0,1:T(4,128)(2,1)} %copy.220), calls=%async_computation.5 | async-start | bytes 3407872 | tf_op jit(solution)/shard_map/all_to_all | solution.py:260
  407.4 4.7 %copy-start.4 = (f32[52,8,8,128]{3,2,1,0:T(8,128)S(1)}, f32[52,8,8,128]{3,2,1,0:T(8,128)}, u32[]{:S(2)}) copy-start(f32[52,8,8,128]{3,2,1,0:T(8,128)} %copy-done.3) | copy-start | bytes 5111812
  407.4 4.7 %copy-start.36 = (f32[128]{0:T(128)S(1)}, f32[128]{0:T(128)}, u32[]{:S(2)}) copy-start(f32[128]{0:T(128)} %param.14) | copy-start | bytes 1540
  409.5 3.2 copy-start.29
  409.5 3.4 copy-start.19
  415.1 2.8 copy-start.6
  415.1 3.1 copy-start.33
  415.1 3.1 copy-start.15
  415.2 3.1 copy-start.31
  416.4 3.2 copy-start.1
  (6 other events, 5.6 us)
Sparse Core Ops, SparseCore 0:
  25.9 48.7 all-gather.2
  78.1 47.8 all-gather.4
  187.8 82.9 all-reduce.1
  318.7 42.6 reduce-scatter.3
where the time goes:
time: 434 us; the launch traced here: 427 us
  waiting for transfers between devices  128 us (29%)
  local copies, waits for them, and re-layouts  109 us (25%)
  matrix products  85 us (20%)
  other arithmetic  36.4 us (8%)
  starting transfers between devices  32.3 us (7%)
  blocking collectives  19.6 us (5%)
  between operations  15.7 us (4%)
    psum x1, waiting for transfers between devices, shards(): lax.psum(part_weighted.astype(jnp.bfloat16), 'seq').astype(jnp.float32)  28.4 us
    unnamed x92, local copies, waits for them, and re-layouts  26.6 us
    psum x1, blocking collectives, shards(): lax.psum(part_sum.astype(jnp.bfloat16), 'seq').astype(jnp.float32)  19.6 us
    all_to_all x1, waiting for transfers between devices, shards(): lax.all_to_all(back_keys, 'conv', split_axis=0, concat_axis=0, tiled=True)  17.5 us
    all_to_all x1, waiting for transfers between devices, shards(): lax.all_to_all(lax.all_to_all(outgoing_keys, 'conv', split_axis=0, concat...  17.2 us
    all_to_all x1, waiting for transfers between devices, shards(): lax.all_to_all(send_values, 'conv', split_axis=0, concat_axis=0, tiled=True)  17.2 us
    all_to_all x1, waiting for transfers between devices, shards(): lax.all_to_all(lax.all_to_all(back_values, 'conv', split_axis=0, concat_a...  16.7 us
    all_to_all x1, waiting for transfers between devices, shards(): lax.all_to_all(outgoing_keys, 'conv', split_axis=0, concat_axis=0, tiled=...  16.1 us
  transfers between devices with their start and end apart: 12, of which 8 were waited for; matrix products, arithmetic and copies ran while one was open for 45% of the time, Pallas kernels for 0%

commit v1 on v0

--- a/solution.py
+++ b/solution.py
@@ -4,6 +4,8 @@
 import jax
 import jax.numpy as jnp
 from jax import lax
+from jax.experimental import pallas as pl
+from jax.experimental.pallas import tpu as pltpu
 from jax.sharding import PartitionSpec as P
 
 TILE = 1601
@@ -149,7 +151,7 @@
     return (grad_query, jnp.stack(key_parts, axis=1), jnp.stack(value_parts, axis=1))
 
 
-def shards(queries, keys, values, q_gain, k_gain, gate, tile_count, tile_owner, visible, d_out):
+def row_shards(queries, keys, values, q_gain, k_gain, gate, tile_count, tile_owner, visible, d_out):
     conv_count = lax.axis_size("conv")
     tensor_count = lax.axis_size("tensor")
     conv_index = lax.axis_index("conv")
@@ -285,6 +287,251 @@
     return (attended, d_queries, d_keys, d_values)
 
 
+LOG2E = math.log2(math.e)
+
+
+def row_chunks(rows):
+    starts = list(range(0, max(rows - 511, 1), 512))
+    return [(a, b - a) for a, b in zip(starts, starts[1:] + [rows])]
+
+
+def inverse_rms(inputs):
+    return lax.rsqrt(jnp.mean(inputs * inputs, axis=-1, keepdims=True) + EPSILON)
+
+
+def norm_back(inputs, inv, gained):
+    return inv * gained - inputs * (inv * inv * inv) * jnp.mean(
+        inputs * gained, axis=-1, keepdims=True
+    )
+
+
+def dot(lhs, rhs):
+    return jnp.dot(lhs, rhs, preferred_element_type=jnp.float32)
+
+
+def prepare_tile(tile, k_raw, v_raw, k_gain, kn, kt, vt):
+    rows = k_raw.shape[1]
+    for start in range(0, rows, 128):
+        at = pl.ds(start, 128)
+        raw = k_raw[tile, at, :].astype(jnp.float32)
+        normed = raw * inverse_rms(raw) * k_gain
+        kn[tile, at, :] = normed.astype(jnp.bfloat16)
+        kt[tile, :, at] = normed.T.astype(jnp.bfloat16)
+        vt[tile, :, at] = v_raw[tile, at, :].astype(jnp.float32).T.astype(jnp.bfloat16)
+
+
+def finish_tile(tile, k_raw, k_gain, dk, dv, dk_out, dv_out):
+    rows = k_raw.shape[1]
+    for start in range(0, rows, 128):
+        at = pl.ds(start, 128)
+        raw = k_raw[tile, at, :].astype(jnp.float32)
+        grad = dk[tile, at, :] * (1.0 / LOG2E) * k_gain
+        dk_out[tile, at, :] = norm_back(raw, inverse_rms(raw), grad).astype(jnp.bfloat16)
+        dv_out[tile, at, :] = dv[tile, at, :].astype(jnp.bfloat16)
+
+
+def attend_block(
+    block, last_seen, tiles, q_raw, d_out, seen, gate_value, q_gain, v_raw, kn, kt, vt,
+    att_out, dq_out, wts, qs, qst, dos, dost, acc, total, dqt, dk, dv,
+):
+    size = q_gain.shape[1]
+    group = q_raw.shape[1] // size
+    count = seen.shape[2] // group
+    rows = v_raw.shape[1]
+    chunks = row_chunks(rows)
+    scale = 1.0 / math.sqrt(size)
+    at = pl.ds(pl.multiple_of(block * count, count), count)
+    for g in range(group):
+        raw = q_raw[at, pl.ds(g * size, size)].astype(jnp.float32)
+        normed = raw * inverse_rms(raw) * (q_gain * (scale * LOG2E))
+        qs[pl.ds(g * count, count), :] = normed.astype(jnp.bfloat16)
+        qst[:, pl.ds(g * count, count)] = normed.T.astype(jnp.bfloat16)
+    seen_row = seen[block]
+    acc[...] = jnp.zeros_like(acc)
+    total[...] = jnp.zeros_like(total)
+    dqt[...] = jnp.zeros_like(dqt)
+
+    for tile in range(tiles):
+        @pl.when(last_seen > tile)
+        def _(tile=tile):
+            mask = (seen_row > tile).astype(jnp.float32)
+            part = jnp.zeros(acc.shape, jnp.float32)
+            part_sum = jnp.zeros(total.shape, jnp.float32)
+            for start, length in chunks:
+                here = pl.ds(start, length)
+                w = jnp.exp2(dot(kn[tile, here, :], qst[...]))
+                if start + length > TILE:
+                    ids = start + lax.broadcasted_iota(jnp.int32, w.shape, 0)
+                    w = jnp.where(ids < TILE, w, 0.0)
+                part_sum = part_sum + jnp.sum(w, axis=0, keepdims=True)
+                w_bf = w.astype(jnp.bfloat16)
+                wts[tile, here, :] = w_bf
+                part = part + dot(vt[tile, :, here], w_bf)
+            acc[...] += part * mask
+            total[...] += part_sum * mask
+
+    safe = jnp.where(total[...] > 0, total[...], 1.0)
+    inv = 1.0 / safe
+    ctx = acc[...] * inv
+    for g in range(group):
+        lanes = pl.ds(g * count, count)
+        grad = d_out[at, pl.ds(g * size, size)].astype(jnp.float32) * gate_value
+        dost[:, lanes] = grad.T
+        att_out[at, pl.ds(g * size, size)] = (
+            (gate_value * ctx[:, g * count:(g + 1) * count]).T.astype(jnp.bfloat16)
+        )
+    scaled = (dost[...] * inv).astype(jnp.bfloat16)
+    scaled32 = scaled.astype(jnp.float32)
+    delta = jnp.sum(scaled32 * ctx, axis=0, keepdims=True)
+
+    for tile in range(tiles):
+        @pl.when(last_seen > tile)
+        def _(tile=tile):
+            mask = (seen_row > tile).astype(jnp.float32)
+            cut32 = scaled32 * mask
+            cut = cut32.astype(jnp.bfloat16)
+            for g in range(group):
+                dos[pl.ds(g * count, count), :] = (
+                    cut32[:, g * count:(g + 1) * count].T.astype(jnp.bfloat16)
+                )
+            low = delta * mask
+            part = jnp.zeros(dqt.shape, jnp.float32)
+            for start, length in chunks:
+                here = pl.ds(start, length)
+                w_bf = wts[tile, here, :]
+                dp = dot(v_raw[tile, here, :], cut)
+                ds = (w_bf.astype(jnp.float32) * (dp - low)).astype(jnp.bfloat16)
+                dv[tile, here, :] += dot(w_bf, dos[...])
+                dk[tile, here, :] += dot(ds, qs[...])
+                part = part + dot(kt[tile, :, here], ds)
+            dqt[...] += part
+
+    for g in range(group):
+        raw = q_raw[at, pl.ds(g * size, size)].astype(jnp.float32)
+        grad = dqt[:, pl.ds(g * count, count)].T * (q_gain * scale)
+        dq_out[at, pl.ds(g * size, size)] = norm_back(raw, inverse_rms(raw), grad).astype(
+            jnp.bfloat16
+        )
+
+
+def head_kernel(
+    last, counts, gate, q_raw, d_out, k_raw, v_raw, seen, q_gain_ref, k_gain_ref,
+    att_out, dq_out, dk_out, dv_out,
+    kn, kt, vt, wts, qs, qst, dos, dost, acc, total, dqt, dk, dv,
+):
+    tiles = k_raw.shape[0]
+    q_gain = q_gain_ref[...]
+    k_gain = k_gain_ref[...]
+    dk[...] = jnp.zeros_like(dk)
+    dv[...] = jnp.zeros_like(dv)
+    for tile in range(tiles):
+        prepare_tile(tile, k_raw, v_raw, k_gain, kn, kt, vt)
+
+    @pl.loop(0, seen.shape[0])
+    def _(block):
+        attend_block(
+            block, last[block], tiles, q_raw, d_out, seen, gate[0], q_gain, v_raw, kn, kt, vt,
+            att_out, dq_out, wts, qs, qst, dos, dost, acc, total, dqt, dk, dv,
+        )
+
+    for tile in range(tiles):
+        finish_tile(tile, k_raw, k_gain, dk, dv, dk_out, dv_out)
+
+
+def core_scratch(tiles, rows, size, lanes):
+    bf, f32 = jnp.bfloat16, jnp.float32
+    return [
+        pltpu.VMEM((tiles, rows, size), bf),
+        pltpu.VMEM((tiles, size, rows), bf),
+        pltpu.VMEM((tiles, size, rows), bf),
+        pltpu.VMEM((tiles, rows, lanes), bf),
+        pltpu.VMEM((lanes, size), bf),
+        pltpu.VMEM((size, lanes), bf),
+        pltpu.VMEM((lanes, size), bf),
+        pltpu.VMEM((size, lanes), f32),
+        pltpu.VMEM((size, lanes), f32),
+        pltpu.VMEM((1, lanes), f32),
+        pltpu.VMEM((size, lanes), f32),
+        pltpu.VMEM((tiles, rows, size), f32),
+        pltpu.VMEM((tiles, rows, size), f32),
+    ]
+
+
+def head_shards(queries, keys, values, q_gain, k_gain, gate, tile_count, tile_owner, visible, d_out):
+    conv_count = lax.axis_size("conv")
+    tensor_count = lax.axis_size("tensor")
+    seq_count = lax.axis_size("seq")
+    conv_index = lax.axis_index("conv")
+    slot_count, row_local, features = keys.shape
+    size = q_gain.shape[0]
+    block_tokens, width = queries.shape[1:]
+    group = width // (features // tensor_count)
+    lanes = group * block_tokens
+    everyone = ("conv", "seq", "tensor")
+
+    own_owners = lax.dynamic_index_in_dim(tile_owner, conv_index, 0, keepdims=False)
+    own_count = lax.dynamic_index_in_dim(tile_count, conv_index, 0, keepdims=False)
+    seen = jnp.minimum(lax.dynamic_index_in_dim(visible, conv_index, 0, keepdims=False), own_count)
+    seen = seen.reshape(seq_count, 1, block_tokens)
+    last = seen[:, 0, -1]
+    seen = jnp.tile(seen, (1, 1, group))
+
+    both = jnp.stack([queries[0], d_out[0]]).reshape(2, block_tokens, seq_count, width // seq_count)
+    both = lax.all_to_all(both, "seq", split_axis=2, concat_axis=1, tiled=True)
+    both = both.reshape(2, seq_count * block_tokens, width // seq_count)
+
+    goes = tile_owner == conv_index
+    slot_of = jnp.argmax(goes, axis=1)
+    pair = jnp.stack([keys, values], axis=2).reshape(
+        slot_count, row_local, 2, tensor_count, seq_count, size
+    )
+    pair = jnp.transpose(pair, (0, 4, 3, 1, 2, 5))
+    sent = jnp.take(pair, slot_of, axis=0).reshape(-1, row_local, 2, size)
+    got = lax.all_to_all(sent, everyone, split_axis=0, concat_axis=0, tiled=True)
+    got = got.reshape(conv_count, -1, 2, size)
+    mine = jnp.take(got, jnp.maximum(own_owners, 0), axis=0)
+    rows = mine.shape[1]
+
+    vmem = pl.BlockSpec(memory_space=pltpu.VMEM)
+    smem = pl.BlockSpec(memory_space=pltpu.SMEM)
+    att, dq, dk, dv = pl.pallas_call(
+        head_kernel,
+        out_shape=[jax.ShapeDtypeStruct(both.shape[1:], jnp.bfloat16)] * 2
+        + [jax.ShapeDtypeStruct((slot_count, rows, size), jnp.bfloat16)] * 2,
+        in_specs=[smem] * 3 + [vmem] * 7,
+        out_specs=[vmem] * 4,
+        scratch_shapes=core_scratch(slot_count, rows, size, lanes),
+        compiler_params=pltpu.CompilerParams(vmem_limit_bytes=60 << 20),
+    )(
+        last, own_count.reshape(1), jnp.tanh(gate), both[0], both[1], mine[:, :, 0], mine[:, :, 1],
+        seen, q_gain[None], k_gain[None],
+    )
+
+    outs = jnp.stack([att, dq]).reshape(2, seq_count, block_tokens, width // seq_count)
+    outs = lax.all_to_all(outs, "seq", split_axis=1, concat_axis=3, tiled=True)
+    attended = outs[0].reshape(1, block_tokens, width)
+    d_queries = outs[1].reshape(1, block_tokens, width)
+
+    tile_of = jnp.argmax(own_owners[None, :] == jnp.arange(conv_count)[:, None], axis=1)
+    back = jnp.take(jnp.stack([dk, dv], axis=1), tile_of, axis=0)
+    back = back.reshape(conv_count, 2, -1, row_local, size)
+    back = jnp.transpose(back, (0, 2, 1, 3, 4)).reshape(-1, 2, row_local, size)
+    back = lax.all_to_all(back, everyone, split_axis=0, concat_axis=0, tiled=True)
+    back = back.reshape(conv_count, seq_count, tensor_count, 2, row_local, size)
+    taker = jnp.argmax(goes, axis=0)
+    used = jnp.any(goes, axis=0)
+    back = jnp.take(back, taker, axis=0)
+    back = jnp.transpose(back, (3, 0, 4, 2, 1, 5)).reshape(2, slot_count, row_local, features)
+    back = jnp.where(used[None, :, None, None], back, jnp.zeros((), jnp.bfloat16))
+    return (attended, d_queries, back[0], back[1])
+
+
+def shards(queries, keys, *rest):
+    heads = keys.shape[2] // rest[1].shape[0]
+    split = lax.axis_size("seq") * lax.axis_size("tensor")
+    return (head_shards if heads == split else row_shards)(queries, keys, *rest)
+
+
 def solution(mesh):
     in_specs = (
         P("conv", "seq", "tensor"),

time: 434 us -> 269 us (0.62); the launches traced: 427 us -> 267 us
  matrix products: 85 us -> 0 us
  local copies, waits for them, and re-layouts: 109 us -> 37.6 us
  waiting for transfers between devices: 128 us -> 170 us
  blocking collectives: 19.6 us -> 0 us
  other arithmetic: 36.4 us -> 20.6 us
  Pallas kernels: 0 us -> 14.9 us
  between operations: 15.7 us -> 1.51 us
  starting transfers between devices: 32.3 us -> 22.7 us
    dot_general x20 -> x0, matrix products: 85 us -> none  [the longest x2 15 us: tile_weights(): jnp.einsum('pkgd,rkd->kgpr', query_bf, key_tile, preferred_element_type=j...]
    all_to_all x8 -> x4, waiting for transfers between devices: 99.7 us -> 170 us  [the longest x1 72.4 us: head_shards(): lax.all_to_all(sent, everyone, split_axis=0, concat_axis=0, tiled=True)]
    all_to_all x10 -> x2, local copies, waits for them, and re-layouts: 44.7 us -> 2.5 us  [the longest x1 2.28 us: head_shards(): outs = lax.all_to_all(outs, 'seq', split_axis=1, concat_axis=3, tiled=True)]
    psum x1 -> x0, waiting for transfers between devices: 28.4 us -> none  [shards(): lax.psum(part_weighted.astype(jnp.bfloat16), 'seq').astype(jnp.float32)]
    psum x1 -> x0, blocking collectives: 19.6 us -> none  [shards(): lax.psum(part_sum.astype(jnp.bfloat16), 'seq').astype(jnp.float32)]
    unnamed x92 -> x17, local copies, waits for them, and re-layouts: 26.6 us -> 9.82 us
    unnamed x1 -> x0, other arithmetic: 15.6 us -> none
    pallas_call x0 -> x1, Pallas kernels: none -> 14.9 us  [head_shards(): pl.pallas_call(head_kernel, out_shape=[jax.ShapeDtypeStruct(both.shape[1:...]
  transfers between devices with their start and end apart: 12 -> 4, of which waited for: 8 -> 4; matrix products, arithmetic and copies ran while one was open for 45% -> 13% of each run, Pallas kernels for 0% -> 0%
where the time goes in v1:
time: 269 us; the launch traced here: 267 us
  waiting for transfers between devices  170 us (63%)
  local copies, waits for them, and re-layouts  37.6 us (14%)
  starting transfers between devices  22.7 us (8%)
  other arithmetic  20.6 us (8%)
  Pallas kernels  14.9 us (6%)
    all_to_all x1, waiting for transfers between devices, head_shards(): lax.all_to_all(sent, everyone, split_axis=0, concat_axis=0, tiled=True)  72.4 us
    all_to_all x1, waiting for transfers between devices, head_shards(): lax.all_to_all(back, everyone, split_axis=0, concat_axis=0, tiled=True)  68.7 us
    all_to_all x1, waiting for transfers between devices, head_shards(): outs = lax.all_to_all(outs, 'seq', split_axis=1, concat_axis=3, tiled=True)  17.1 us
    pallas_call x1, Pallas kernels, head_shards(): pl.pallas_call(head_kernel, out_shape=[jax.ShapeDtypeStruct(both.shape[1:...  14.9 us
    all_to_all x1, waiting for transfers between devices, head_shards(): both = lax.all_to_all(both, 'seq', split_axis=2, concat_axis=1, tiled=True)  12 us
    unnamed x17, local copies, waits for them, and re-layouts  9.82 us
    all_to_all x1, starting transfers between devices, head_shards(): lax.all_to_all(back, everyone, split_axis=0, concat_axis=0, tiled=True)  8.87 us
    all_to_all x1, starting transfers between devices, head_shards(): both = lax.all_to_all(both, 'seq', split_axis=2, concat_axis=1, tiled=True)  6.48 us
  transfers between devices with their start and end apart: 4, of which 4 were waited for; matrix products, arithmetic and copies ran while one was open for 13% of the time, Pallas kernels for 0%

profile of v1, /device:TPU:0, one launch (start us, length us, event | category | flops | bytes accessed | tf_op | source)
XLA Modules:
  0.0 267.5 jit_solution(6401160567169192727)
XLA Ops:
  0.6 1.3 copy.71
  1.9 1.3 copy.72
  3.4 1.3 copy.73
  4.7 6.5 %all-to-all-start = ((bf16[2,128,4,512]{3,1,0,2:T(8,128)(2,1)}), bf16[2,128,4,512]{3,1,0,2:T(8,128)(2,1)S(1)}, u32[]{:S(2)}, u32[]{:S(2)}) async-start(bf16[2,128,4,512]{3,1,0,2:T(8,128)(2,1)} %copy.73), calls=%async_computation | async-start | bytes 2097152 | tf_op jit(solution)/shard_map/all_to_all | solution.py:480
  11.3 0.6 stack.31
  11.9 1.0 copy.74
  12.9 0.4 copy-done.3
  13.4 0.6 stack.32
  14.0 1.0 copy.75
  15.2 0.6 compare_reduce_fusion
  15.8 0.5 iota_reduce_fusion.1
  16.5 1.6 maximum_bitcast_fusion
  18.1 2.7 %gather_fusion = bf16[4,4,2,208,2,128]{5,3,4,2,1,0:T(8,128)(2,1)} fusion(bf16[2,4,2,208,2,128]{5,3,4,2,1,0:T(8,128)(2,1)S(1)} %maximum_bitcast_fusion, s32[1024]{0:T(1024)S(1)} %pad_clamp_fusion.3), kind=kCustom, calls=%fused_computation | custom fusion | bytes 6815760 | tf_op jit(solution)/shard_map/jit(_take)/gather | solution.py:489
  20.8 4.1 %bitcast_select_fusion = bf16[32,208,2,128]{3,1,2,0:T(8,128)(2,1)} fusion(bf16[4,4,2,208,2,128]{5,3,4,2,1,0:T(8,128)(2,1)} %gather_fusion, pred[32]{0:T(512)(128)(4,1)S(1)} %broadcast_in_dim.73), kind=kLoop, calls=%fused_computation.4 | loop fusion | flops 1703936 | bytes 6815776 | tf_op jit(solution)/shard_map/jit(_take)/select_n | solution.py:489
  24.9 12.0 %all-to-all-done = bf16[2,128,4,512]{3,1,0,2:T(8,128)(2,1)S(1)} async-done(((bf16[2,128,4,512]{3,1,0,2:T(8,128)(2,1)}), bf16[2,128,4,512]{3,1,0,2:T(8,128)(2,1)S(1)}, u32[]{:S(2)}, u32[]{:S(2)}) %all-to-all-start) | async-done | bytes 1048608 | tf_op jit(solution)/shard_map/all_to_all | solution.py:480
  36.9 1.0 copy-done
  37.9 3.9 %all-to-all-start.1 = ((bf16[32,208,2,128]{3,1,2,0:T(8,128)(2,1)}), bf16[32,208,2,128]{3,1,2,0:T(8,128)(2,1)S(1)}, u32[]{:S(2)}, u32[]{:S(2)}) async-start(bf16[32,208,2,128]{3,1,2,0:T(8,128)(2,1)} %bitcast_select_fusion), calls=%async_computation.1 | async-start | bytes 6815744 | tf_op jit(solution)/shard_map/all_to_all | solution.py:490
  41.8 0.6 dynamic_slice.13.counts
  42.4 1.3 dynamic-slice_minimum_fusion
  43.8 0.7 copy.86
  45.2 2.2 fusion.2
  47.4 72.4 %all-to-all-done.1 = bf16[32,208,2,128]{3,1,2,0:T(8,128)(2,1)S(1)} async-done(((bf16[32,208,2,128]{3,1,2,0:T(8,128)(2,1)}), bf16[32,208,2,128]{3,1,2,0:T(8,128)(2,1)S(1)}, u32[]{:S(2)}, u32[]{:S(2)}) %all-to-all-start.1) | async-done | bytes 3407904 | tf_op jit(solution)/shard_map/all_to_all | solution.py:490
  119.8 0.2 copy.76
  120.0 0.2 copy.77
  120.2 2.0 gather_fusion.1
  122.2 1.7 copy_select_fusion.1
  123.9 1.3 slice_bitcast_fusion.2
  125.2 0.6 tile.8
  125.8 14.9 %shard_map.129 = (bf16[512,512]{1,0:T(8,128)(2,1)}, bf16[512,512]{1,0:T(8,128)(2,1)}, bf16[2,1664,128]{2,1,0:T(8,128)(2,1)}, bf16[2,1664,128]{2,1,0:T(8,128)(2,1)}) custom-call(s32[4]{0:T(128)} %bitcast.63, s32[1]{0:T(128)} %dynamic_slice.13.counts, f32[1]{0:T(128)S(6)} %tanh.3.gate, bf16[512,512]{1,0:T(8,128)(2,1)} %bitcast.55, bf16[512,512]{1,0:T(8,128)(2,1)} %bitcast.54, ...), custom_call_target="tpu_custom_call" | custom-call | tf_op jit(solution)/shard_map/pallas_call | solution.py:497
  140.7 2.3 pad_maximum_fusion.2
  142.9 3.5 %all-to-all-start.2 = ((bf16[2,4,128,512]{3,2,0,1:T(8,128)(2,1)}), bf16[2,4,128,512]{3,2,0,1:T(8,128)(2,1)S(1)}, u32[]{:S(2)}, u32[]{:S(2)}) async-start(bf16[2,4,128,512]{3,2,0,1:T(8,128)(2,1)} %pad_maximum_fusion.2), calls=%async_computation.2 | async-start | bytes 2097152 | tf_op jit(solution)/shard_map/all_to_all | solution.py:511
  146.5 1.6 pad_maximum_fusion
  148.1 2.7 %gather_fusion.2 = bf16[4,2,1664,128]{3,2,1,0:T(8,128)(2,1)} fusion(bf16[2,2,1664,128]{3,2,0,1:T(8,128)(2,1)S(1)} %pad_maximum_fusion, s32[1024]{0:T(1024)S(1)} %pad_clamp_fusion.1), kind=kCustom, calls=%fused_computation.2 | custom fusion | bytes 6815760 | tf_op jit(solution)/shard_map/jit(_take)/gather | solution.py:516
  150.8 4.1 %copy_select_fusion = bf16[4,2,8,208,128]{4,3,1,2,0:T(8,128)(2,1)} fusion(bf16[4,2,8,208,128]{4,3,2,1,0:T(8,128)(2,1)} %bitcast.46, pred[4]{0:T(512)(128)(4,1)S(1)} %get-tuple-element.40), kind=kLoop, calls=%fused_computation.5 | loop fusion | flops 1703936 | bytes 6815748 | tf_op jit(solution)/shard_map/jit(_take)/select_n | solution.py:516
  154.9 17.1 %all-to-all-done.2 = bf16[2,4,128,512]{3,2,0,1:T(8,128)(2,1)S(1)} async-done(((bf16[2,4,128,512]{3,2,0,1:T(8,128)(2,1)}), bf16[2,4,128,512]{3,2,0,1:T(8,128)(2,1)S(1)}, u32[]{:S(2)}, u32[]{:S(2)}) %all-to-all-start.2) | async-done | bytes 1048608 | tf_op jit(solution)/shard_map/all_to_all | solution.py:511
  172.0 1.0 copy-done.1
  173.0 8.9 %all-to-all-start.3 = ((bf16[32,2,208,128]{3,2,1,0:T(8,128)(2,1)}), bf16[32,2,208,128]{3,2,1,0:T(8,128)(2,1)S(1)}, u32[]{:S(2)}, u32[]{:S(2)}) async-start(bf16[32,2,208,128]{3,2,1,0:T(8,128)(2,1)} %bitcast.31), calls=%async_computation.3 | async-start | bytes 6815744 | tf_op jit(solution)/shard_map/all_to_all | solution.py:519
  181.8 0.6 iota_reduce_fusion
  182.5 2.3 copy.81
  184.8 2.2 fusion.1
  187.0 2.0 copy.84
  189.1 2.0 copy.85
  191.1 68.7 %all-to-all-done.3 = bf16[32,2,208,128]{3,2,1,0:T(8,128)(2,1)S(1)} async-done(((bf16[32,2,208,128]{3,2,1,0:T(8,128)(2,1)}), bf16[32,2,208,128]{3,2,1,0:T(8,128)(2,1)S(1)}, u32[]{:S(2)}, u32[]{:S(2)}) %all-to-all-start.3) | async-done | bytes 3407904 | tf_op jit(solution)/shard_map/all_to_all | solution.py:519
  259.8 2.0 gather_fusion.3
  261.7 1.7 select_bitcast_fusion
  263.4 1.3 copy.83
  264.7 1.2 reshape.112
  266.2 1.3 slice_bitcast_fusion
  (25 shorter events, 0.9 us)
Async XLA Ops:
  3.4 7.8 %copy-start.4 = (s32[4,2]{0,1:T(2,128)S(1)}, s32[4,2]{0,1:T(2,128)}, u32[]{:S(2)}) copy-start(s32[4,2]{0,1:T(2,128)} %param.17) | copy-start | bytes 100
  4.7 6.6 %copy-start.2 = (bf16[2,208,1024]{2,1,0:T(8,128)(2,1)S(1)}, bf16[2,208,1024]{2,1,0:T(8,128)(2,1)}, u32[]{:S(2)}) copy-start(bf16[2,208,1024]{2,1,0:T(8,128)(2,1)} %param.11) | copy-start | bytes 2555908
  4.7 32.2 %all-to-all-start = ((bf16[2,128,4,512]{3,1,0,2:T(8,128)(2,1)}), bf16[2,128,4,512]{3,1,0,2:T(8,128)(2,1)S(1)}, u32[]{:S(2)}, u32[]{:S(2)}) async-start(bf16[2,128,4,512]{3,1,0,2:T(8,128)(2,1)} %copy.73), calls=%async_computation | async-start | bytes 2097152 | tf_op jit(solution)/shard_map/all_to_all | solution.py:480
  11.9 1.4 copy-start.3
  24.9 16.9 %copy-start.5 = (s32[4]{0:T(128)S(1)}, s32[4]{0:T(128)}, u32[]{:S(2)}) copy-start(s32[4]{0:T(128)} %param.16) | copy-start | bytes 52
  36.9 1.0 copy-start
  37.9 81.9 %all-to-all-start.1 = ((bf16[32,208,2,128]{3,1,2,0:T(8,128)(2,1)}), bf16[32,208,2,128]{3,1,2,0:T(8,128)(2,1)S(1)}, u32[]{:S(2)}, u32[]{:S(2)}) async-start(bf16[32,208,2,128]{3,1,2,0:T(8,128)(2,1)} %bitcast_select_fusion), calls=%async_computation.1 | async-start | bytes 6815744 | tf_op jit(solution)/shard_map/all_to_all | solution.py:490
  142.9 29.0 %all-to-all-start.2 = ((bf16[2,4,128,512]{3,2,0,1:T(8,128)(2,1)}), bf16[2,4,128,512]{3,2,0,1:T(8,128)(2,1)S(1)}, u32[]{:S(2)}, u32[]{:S(2)}) async-start(bf16[2,4,128,512]{3,2,0,1:T(8,128)(2,1)} %pad_maximum_fusion.2), calls=%async_computation.2 | async-start | bytes 2097152 | tf_op jit(solution)/shard_map/all_to_all | solution.py:511
  172.0 1.0 copy-start.1
  173.0 86.8 %all-to-all-start.3 = ((bf16[32,2,208,128]{3,2,1,0:T(8,128)(2,1)}), bf16[32,2,208,128]{3,2,1,0:T(8,128)(2,1)S(1)}, u32[]{:S(2)}, u32[]{:S(2)}) async-start(bf16[32,2,208,128]{3,2,1,0:T(8,128)(2,1)} %bitcast.31), calls=%async_computation.3 | async-start | bytes 6815744 | tf_op jit(solution)/shard_map/all_to_all | solution.py:519

commit v2 on v1

--- a/solution.py
+++ b/solution.py
@@ -457,6 +457,21 @@
     ]
 
 
+def move_convs(outgoing):
+    count = len(outgoing)
+    return [outgoing[0]] + [
+        lax.ppermute(outgoing[shift], "conv", [(i, (i + shift) % count) for i in range(count)])
+        for shift in range(1, count)
+    ]
+
+
+def choose(arrived, index):
+    chosen = arrived[0]
+    for shift in range(1, len(arrived)):
+        chosen = jnp.where(index == shift, arrived[shift], chosen)
+    return chosen
+
+
 def head_shards(queries, keys, values, q_gain, k_gain, gate, tile_count, tile_owner, visible, d_out):
     conv_count = lax.axis_size("conv")
     tensor_count = lax.axis_size("tensor")
@@ -482,15 +497,26 @@
 
     goes = tile_owner == conv_index
     slot_of = jnp.argmax(goes, axis=1)
-    pair = jnp.stack([keys, values], axis=2).reshape(
-        slot_count, row_local, 2, tensor_count, seq_count, size
-    )
-    pair = jnp.transpose(pair, (0, 4, 3, 1, 2, 5))
-    sent = jnp.take(pair, slot_of, axis=0).reshape(-1, row_local, 2, size)
-    got = lax.all_to_all(sent, everyone, split_axis=0, concat_axis=0, tiled=True)
-    got = got.reshape(conv_count, -1, 2, size)
-    mine = jnp.take(got, jnp.maximum(own_owners, 0), axis=0)
-    rows = mine.shape[1]
+    shifts = list(range(conv_count))
+    own_shift = jnp.remainder(conv_index - own_owners, conv_count)
+
+    def fetch(stored):
+        outgoing = [
+            lax.dynamic_index_in_dim(
+                stored, slot_of[jnp.remainder(conv_index + shift, conv_count)], 0, keepdims=False
+            )
+            for shift in shifts
+        ]
+        arrived = move_convs(outgoing)
+        mine = jnp.stack([choose(arrived, own_shift[tile]) for tile in range(slot_count)])
+        mine = mine.reshape(slot_count, row_local, tensor_count, seq_count, size)
+        mine = jnp.transpose(mine, (3, 2, 0, 1, 4)).reshape(-1, slot_count, row_local, size)
+        mine = lax.all_to_all(mine, ("seq", "tensor"), split_axis=0, concat_axis=0, tiled=True)
+        return jnp.transpose(mine, (1, 0, 2, 3)).reshape(slot_count, -1, size)
+
+    key_tiles = fetch(keys)
+    value_tiles = fetch(values)
+    rows = key_tiles.shape[1]
 
     vmem = pl.BlockSpec(memory_space=pltpu.VMEM)
     smem = pl.BlockSpec(memory_space=pltpu.SMEM)
@@ -503,27 +529,44 @@
         scratch_shapes=core_scratch(slot_count, rows, size, lanes),
         compiler_params=pltpu.CompilerParams(vmem_limit_bytes=60 << 20),
     )(
-        last, own_count.reshape(1), jnp.tanh(gate), both[0], both[1], mine[:, :, 0], mine[:, :, 1],
+        last, own_count.reshape(1), jnp.tanh(gate), both[0], both[1], key_tiles, value_tiles,
         seen, q_gain[None], k_gain[None],
     )
 
-    outs = jnp.stack([att, dq]).reshape(2, seq_count, block_tokens, width // seq_count)
+    tile_of = jnp.argmax(own_owners[None, :] == jnp.arange(conv_count)[:, None], axis=1)
+    taker = jnp.argmax(goes, axis=0)
+    used = jnp.any(goes, axis=0)
+    taker_shift = jnp.remainder(conv_index - taker, conv_count)
+
+    def give_back(grads):
+        grads = jnp.transpose(grads.reshape(slot_count, -1, row_local, size), (1, 0, 2, 3))
+        grads = lax.all_to_all(grads, ("seq", "tensor"), split_axis=0, concat_axis=0, tiled=True)
+        grads = grads.reshape(seq_count, tensor_count, slot_count, row_local, size)
+        grads = jnp.transpose(grads, (2, 3, 1, 0, 4)).reshape(slot_count, row_local, features)
+        outgoing = [
+            lax.dynamic_index_in_dim(
+                grads, tile_of[jnp.remainder(conv_index + shift, conv_count)], 0, keepdims=False
+            )
+            for shift in shifts
+        ]
+        arrived = move_convs(outgoing)
+        zero = jnp.zeros((), jnp.bfloat16)
+        return jnp.stack(
+            [
+                jnp.where(used[slot], choose(arrived, taker_shift[slot]), zero)
+                for slot in range(slot_count)
+            ]
+        )
+
+    d_keys = give_back(dk)
+    outs = jnp.stack([att, dq])
+    outs, d_keys = lax.optimization_barrier((outs, d_keys))
+    outs = outs.reshape(2, seq_count, block_tokens, width // seq_count)
     outs = lax.all_to_all(outs, "seq", split_axis=1, concat_axis=3, tiled=True)
     attended = outs[0].reshape(1, block_tokens, width)
     d_queries = outs[1].reshape(1, block_tokens, width)
 
-    tile_of = jnp.argmax(own_owners[None, :] == jnp.arange(conv_count)[:, None], axis=1)
-    back = jnp.take(jnp.stack([dk, dv], axis=1), tile_of, axis=0)
-    back = back.reshape(conv_count, 2, -1, row_local, size)
-    back = jnp.transpose(back, (0, 2, 1, 3, 4)).reshape(-1, 2, row_local, size)
-    back = lax.all_to_all(back, everyone, split_axis=0, concat_axis=0, tiled=True)
-    back = back.reshape(conv_count, seq_count, tensor_count, 2, row_local, size)
-    taker = jnp.argmax(goes, axis=0)
-    used = jnp.any(goes, axis=0)
-    back = jnp.take(back, taker, axis=0)
-    back = jnp.transpose(back, (3, 0, 4, 2, 1, 5)).reshape(2, slot_count, row_local, features)
-    back = jnp.where(used[None, :, None, None], back, jnp.zeros((), jnp.bfloat16))
-    return (attended, d_queries, back[0], back[1])
+    return (attended, d_queries, d_keys, give_back(dv))
 
 
 def shards(queries, keys, *rest):

time: 269 us -> 225 us (0.84)
  waiting for transfers between devices: 170 us -> 97.4 us
  between operations: 1.51 us -> 24.4 us
  starting transfers between devices: 22.7 us -> 39.5 us
  local copies, waits for them, and re-layouts: 37.6 us -> 26.9 us
  other arithmetic: 20.6 us -> 13 us
  Pallas kernels: 14.9 us -> 20.6 us
    all_to_all x2 -> x4, waiting for transfers between devices: 141 us -> 34.7 us  [the longest x2 19.1 us: give_back(): lax.all_to_all(grads, ('seq', 'tensor'), split_axis=0, concat_axis=0, til...]
    ppermute x0 -> x12, waiting for transfers between devices: none -> 60.1 us  [move_convs(): lax.ppermute(outgoing[shift], 'conv', [(i, (i + shift) % count) for i in...]
    all_to_all x1, waiting for transfers between devices: 17.1 us -> 2.62 us  [head_shards(): outs = lax.all_to_all(outs, 'seq', split_axis=1, concat_axis=3, tiled=True)]
    all_to_all x1, waiting for transfers between devices: 12 us -> 0.01 us  [head_shards(): both = lax.all_to_all(both, 'seq', split_axis=2, concat_axis=1, tiled=True)]
    select_n x7 -> x3, other arithmetic: 11.7 us -> 2.09 us  [the longest x2 2.08 us: choose(): chosen = jnp.where(index == shift, arrived[shift], chosen)]
    gather x4 -> x0, local copies, waits for them, and re-layouts: 9.41 us -> none  [the longest x1 2.75 us: head_shards(): sent = jnp.take(pair, slot_of, axis=0).reshape(-1, row_local, 2, size)]
    all_to_all x2 -> x4, starting transfers between devices: 12.8 us -> 21.2 us  [the longest x2 12.3 us: fetch(): lax.all_to_all(mine, ('seq', 'tensor'), split_axis=0, concat_axis=0, tile...]
    ppermute x0 -> x12, starting transfers between devices: none -> 7.08 us  [move_convs(): lax.ppermute(outgoing[shift], 'conv', [(i, (i + shift) % count) for i in...]
  transfers between devices with their start and end apart: 4 -> 18, of which waited for: 4 -> 13; matrix products, arithmetic and copies ran while one was open for 13% -> 13% of each run, Pallas kernels for 0% -> 0%
where the time goes in v2:
time: 225 us; the launch traced here: 222 us
  waiting for transfers between devices  97.4 us (43%)
  starting transfers between devices  39.5 us (18%)
  local copies, waits for them, and re-layouts  26.9 us (12%)
  between operations  24.4 us (11%)
  Pallas kernels  20.6 us (9%)
  other arithmetic  13 us (6%)
    ppermute x12, waiting for transfers between devices, move_convs(): lax.ppermute(outgoing[shift], 'conv', [(i, (i + shift) % count) for i in...  60.1 us
    pallas_call x1, Pallas kernels, head_shards(): pl.pallas_call(head_kernel, out_shape=[jax.ShapeDtypeStruct(both.shape[1:...  20.6 us
    all_to_all x2, waiting for transfers between devices, give_back(): lax.all_to_all(grads, ('seq', 'tensor'), split_axis=0, concat_axis=0, til...  19.1 us
    all_to_all x2, waiting for transfers between devices, fetch(): lax.all_to_all(mine, ('seq', 'tensor'), split_axis=0, concat_axis=0, tile...  15.7 us
    all_to_all x2, starting transfers between devices, fetch(): lax.all_to_all(mine, ('seq', 'tensor'), split_axis=0, concat_axis=0, tile...  12.3 us
    all_to_all x2, starting transfers between devices, give_back(): lax.all_to_all(grads, ('seq', 'tensor'), split_axis=0, concat_axis=0, til...  8.89 us
    ppermute x12, starting transfers between devices, move_convs(): lax.ppermute(outgoing[shift], 'conv', [(i, (i + shift) % count) for i in...  7.08 us
    all_to_all x1, starting transfers between devices, head_shards(): both = lax.all_to_all(both, 'seq', split_axis=2, concat_axis=1, tiled=True)  6.48 us
  transfers between devices with their start and end apart: 18, of which 13 were waited for; matrix products, arithmetic and copies ran while one was open for 13% of the time, Pallas kernels for 0%

profile of v2, /device:TPU:0, one launch (start us, length us, event | category | flops | bytes accessed | tf_op | source)
XLA Modules:
  0.0 221.9 jit_solution(4045552178945072713)
XLA Ops:
  0.6 1.4 copy.65
  2.4 1.3 copy.67
  3.7 6.5 %all-to-all-start = ((bf16[2,128,4,512]{3,1,0,2:T(8,128)(2,1)}), bf16[2,128,4,512]{3,1,0,2:T(8,128)(2,1)S(1)}, u32[]{:S(2)}, u32[]{:S(2)}) async-start(bf16[2,128,4,512]{3,1,0,2:T(8,128)(2,1)} %copy.67), calls=%async_computation | async-start | bytes 2097152 | tf_op jit(solution)/shard_map/all_to_all | solution.py:495
  10.2 0.7 copy-done.7
  12.4 0.7 fusion.33
  18.9 1.0 dynamic-slice_bitcast_fusion.6
  19.9 0.7 collective-permute-start.3
  20.6 0.8 collective-permute-start.4
  28.5 2.2 %collective-permute-done.3 = bf16[208,1024]{1,0:T(8,128)(2,1)S(1)} collective-permute-done((bf16[208,1024]{1,0:T(8,128)(2,1)}, bf16[208,1024]{1,0:T(8,128)(2,1)S(1)}, u32[]{:S(2)}, u32[]{:S(2)}) %collective-permute-start.3) | collective-permute-done | bytes 426016 | tf_op jit(solution)/shard_map/ppermute | solution.py:463
  30.7 10.7 %collective-permute-done.4 = bf16[208,1024]{1,0:T(8,128)(2,1)S(1)} collective-permute-done((bf16[208,1024]{1,0:T(8,128)(2,1)}, bf16[208,1024]{1,0:T(8,128)(2,1)S(1)}, u32[]{:S(2)}, u32[]{:S(2)}) %collective-permute-start.4) | collective-permute-done | bytes 426016 | tf_op jit(solution)/shard_map/ppermute | solution.py:463
  42.1 1.2 fusion.17
  44.6 1.0 copy.71
  45.6 6.2 %all-to-all-start.2 = ((bf16[8,2,208,128]{3,2,1,0:T(8,128)(2,1)}), bf16[8,2,208,128]{3,2,1,0:T(8,128)(2,1)S(1)}, u32[]{:S(2)}, u32[]{:S(2)}) async-start(bf16[8,2,208,128]{3,2,1,0:T(8,128)(2,1)} %bitcast.167), calls=%async_computation.2 | async-start | bytes 1703936 | tf_op jit(solution)/shard_map/all_to_all | solution.py:514
  52.4 9.7 %collective-permute-done = bf16[208,1024]{1,0:T(8,128)(2,1)S(1)} collective-permute-done((bf16[208,1024]{1,0:T(8,128)(2,1)S(1)}, bf16[208,1024]{1,0:T(8,128)(2,1)S(1)}, u32[]{:S(2)}, u32[]{:S(2)}) %collective-permute-start) | collective-permute-done | bytes 426016 | tf_op jit(solution)/shard_map/ppermute | solution.py:463
  62.1 9.0 %collective-permute-done.1 = bf16[208,1024]{1,0:T(8,128)(2,1)S(1)} collective-permute-done((bf16[208,1024]{1,0:T(8,128)(2,1)S(1)}, bf16[208,1024]{1,0:T(8,128)(2,1)S(1)}, u32[]{:S(2)}, u32[]{:S(2)}) %collective-permute-start.1) | collective-permute-done | bytes 426016 | tf_op jit(solution)/shard_map/ppermute | solution.py:463
  71.1 0.9 collective-permute-done.2
  72.0 0.9 fusion.21
  72.9 1.3 stack.49
  74.6 1.0 pad_maximum_fusion.2
  75.6 6.1 %all-to-all-start.1 = ((bf16[8,2,208,128]{3,2,1,0:T(8,128)(2,1)}), bf16[8,2,208,128]{3,2,1,0:T(8,128)(2,1)S(1)}, u32[]{:S(2)}, u32[]{:S(2)}) async-start(bf16[8,2,208,128]{3,2,1,0:T(8,128)(2,1)} %bitcast.24), calls=%async_computation.1 | async-start | bytes 1703936 | tf_op jit(solution)/shard_map/all_to_all | solution.py:514
  82.3 1.3 fusion.24
  85.0 1.0 fusion.30
  86.0 1.0 copy.72
  87.0 15.6 %all-to-all-done.1 = bf16[8,2,208,128]{3,2,1,0:T(8,128)(2,1)S(1)} async-done(((bf16[8,2,208,128]{3,2,1,0:T(8,128)(2,1)}), bf16[8,2,208,128]{3,2,1,0:T(8,128)(2,1)S(1)}, u32[]{:S(2)}, u32[]{:S(2)}) %all-to-all-start.1) | async-done | bytes 852000 | tf_op jit(solution)/shard_map/all_to_all | solution.py:514
  102.6 1.0 copy.70
  104.2 20.6 %shard_map.129 = (bf16[512,512]{1,0:T(8,128)(2,1)}, bf16[512,512]{1,0:T(8,128)(2,1)}, bf16[2,1664,128]{2,1,0:T(8,128)(2,1)}, bf16[2,1664,128]{2,1,0:T(8,128)(2,1)}) custom-call(s32[4]{0:T(128)} %bitcast.185, s32[1]{0:T(128)} %dynamic_slice.94.counts, f32[1]{0:T(128)S(6)} %tanh.3.gate, bf16[512,512]{1,0:T(8,128)(2,1)} %bitcast.177, ...), custom_call_target="tpu_custom_call" | custom-call | tf_op jit(solution)/shard_map/pallas_call | solution.py:523
  124.8 2.1 copy.89
  126.9 3.7 %all-to-all-start.3 = ((bf16[8,2,208,128]{3,2,1,0:T(8,128)(2,1)}), bf16[8,2,208,128]{3,2,1,0:T(8,128)(2,1)S(1)}, u32[]{:S(2)}, u32[]{:S(2)}) async-start(bf16[8,2,208,128]{3,2,1,0:T(8,128)(2,1)} %bitcast.160), calls=%async_computation.3 | async-start | bytes 1703936 | tf_op jit(solution)/shard_map/all_to_all | solution.py:543
  130.6 1.0 copy.87
  131.6 19.1 %all-to-all-done.3 = bf16[8,2,208,128]{3,2,1,0:T(8,128)(2,1)S(1)} async-done(((bf16[8,2,208,128]{3,2,1,0:T(8,128)(2,1)}), bf16[8,2,208,128]{3,2,1,0:T(8,128)(2,1)S(1)}, u32[]{:S(2)}, u32[]{:S(2)}) %all-to-all-start.3) | async-done | bytes 852000 | tf_op jit(solution)/shard_map/all_to_all | solution.py:543
  150.6 5.2 %all-to-all-start.5 = ((bf16[8,2,208,128]{3,2,1,0:T(8,128)(2,1)}), bf16[8,2,208,128]{3,2,1,0:T(8,128)(2,1)S(1)}, u32[]{:S(2)}, u32[]{:S(2)}) async-start(bf16[8,2,208,128]{3,2,1,0:T(8,128)(2,1)} %bitcast.158), calls=%async_computation.5 | async-start | bytes 1703936 | tf_op jit(solution)/shard_map/all_to_all | solution.py:543
  162.6 1.1 dynamic-slice_bitcast_fusion.3
  163.7 2.8 %collective-permute-start.7 = (bf16[208,1024]{1,0:T(8,128)(2,1)}, bf16[208,1024]{1,0:T(8,128)(2,1)}, u32[]{:S(2)}, u32[]{:S(2)}) collective-permute-start(bf16[208,1024]{1,0:T(8,128)(2,1)} %get-tuple-element.48), channel_id=1, source_target_pairs={{0,16},{8,24},{16,0},{24,8},{1,17},{9,25},{17,1},{25,9},{2,18},{10... | collective-permute-start | bytes 1277960 | tf_op jit(solution)/shard_map/ppermute | solution.py:463
  173.1 0.7 fusion.31
  173.9 12.2 %collective-permute-done.7 = bf16[208,1024]{1,0:T(8,128)(2,1)} collective-permute-done((bf16[208,1024]{1,0:T(8,128)(2,1)}, bf16[208,1024]{1,0:T(8,128)(2,1)}, u32[]{:S(2)}, u32[]{:S(2)}) %collective-permute-start.7) | collective-permute-done | bytes 426016 | tf_op jit(solution)/shard_map/ppermute | solution.py:463
  186.1 2.6 %fusion.11 = (bf16[1,208,1024]{2,1,0:T(8,128)(2,1)S(1)}, bf16[1,208,1024]{2,1,0:T(8,128)(2,1)S(1)}) fusion(bf16[208,1024]{1,0:T(8,128)(2,1)S(1)} %collective-permute-done.6, bf16[208,1024]{1,0:T(8,128)(2,1)} %collective-permute-done.7, bf16[208,1024]{1,0:T(8,128)(2,1)} %collective-permute-done.8, pred[]{:T(512)} %bitcast.52, pred[]{:T(512)} %bitcast.49, ...), kind=kLoop, calls=%fused_computation.25 | loop fusion | flops 1703936 | bytes 2555916 | tf_op jit(solution)/shard_map/stack | solution.py:554
  188.6 1.0 pad_maximum_fusion.3
  189.6 1.1 copy.75
  190.7 4.7 %all-to-all-start.4 = ((bf16[2,4,128,512]{3,2,0,1:T(8,128)(2,1)}), bf16[2,4,128,512]{3,2,0,1:T(8,128)(2,1)S(1)}, u32[]{:S(2)}, u32[]{:S(2)}) async-start(bf16[2,4,128,512]{3,2,0,1:T(8,128)(2,1)} %copy.75), calls=%async_computation.4 | async-start | bytes 2097152 | tf_op jit(solution)/shard_map/all_to_all | solution.py:565
  197.0 1.7 collective-permute-start.9
  198.8 10.8 %collective-permute-done.10 = bf16[208,1024]{1,0:T(8,128)(2,1)S(1)} collective-permute-done((bf16[208,1024]{1,0:T(8,128)(2,1)S(1)}, bf16[208,1024]{1,0:T(8,128)(2,1)S(1)}, u32[]{:S(2)}, u32[]{:S(2)}) %collective-permute-start.10) | collective-permute-done | bytes 426016 | tf_op jit(solution)/shard_map/ppermute | solution.py:463
  209.6 2.2 collective-permute-done.11
  211.8 2.3 %collective-permute-done.9 = bf16[208,1024]{1,0:T(8,128)(2,1)S(1)} collective-permute-done((bf16[208,1024]{1,0:T(8,128)(2,1)S(1)}, bf16[208,1024]{1,0:T(8,128)(2,1)S(1)}, u32[]{:S(2)}, u32[]{:S(2)}) %collective-permute-start.9) | collective-permute-done | bytes 426016 | tf_op jit(solution)/shard_map/ppermute | solution.py:463
  214.1 1.4 fusion.3
  215.5 1.0 pad_maximum_fusion.4
  216.5 2.6 %all-to-all-done.4 = bf16[2,4,128,512]{3,2,0,1:T(8,128)(2,1)S(1)} async-done(((bf16[2,4,128,512]{3,2,0,1:T(8,128)(2,1)}), bf16[2,4,128,512]{3,2,0,1:T(8,128)(2,1)S(1)}, u32[]{:S(2)}, u32[]{:S(2)}) %all-to-all-start.4) | async-done | bytes 1048608 | tf_op jit(solution)/shard_map/all_to_all | solution.py:565
  219.8 1.0 copy.79
  220.9 1.0 copy.80
  (60 shorter events, 12.5 us)
Async XLA Ops:
  0.6 1.4 copy-start.3
  3.7 15.2 %copy-start = (bf16[2,208,1024]{2,1,0:T(8,128)(2,1)S(1)}, bf16[2,208,1024]{2,1,0:T(8,128)(2,1)}, u32[]{:S(2)}) copy-start(bf16[2,208,1024]{2,1,0:T(8,128)(2,1)} %param.12) | copy-start | bytes 2555908
  3.7 41.8 %all-to-all-start = ((bf16[2,128,4,512]{3,1,0,2:T(8,128)(2,1)}), bf16[2,128,4,512]{3,1,0,2:T(8,128)(2,1)S(1)}, u32[]{:S(2)}, u32[]{:S(2)}) async-start(bf16[2,128,4,512]{3,1,0,2:T(8,128)(2,1)} %copy.67), calls=%async_computation | async-start | bytes 2097152 | tf_op jit(solution)/shard_map/all_to_all | solution.py:495
  10.2 0.7 copy-start.7
  19.9 10.8 %collective-permute-start.3 = (bf16[208,1024]{1,0:T(8,128)(2,1)}, bf16[208,1024]{1,0:T(8,128)(2,1)S(1)}, u32[]{:S(2)}, u32[]{:S(2)}) collective-permute-start(bf16[208,1024]{1,0:T(8,128)(2,1)} %get-tuple-element.52), channel_id=1, source_target_pairs={{0,24},{8,0},{16,8},{24,16},{1,25},{9,1},{17,9},{25,17},{2,26},{10... | collective-permute-start | bytes 1277960 | tf_op jit(solution)/shard_map/ppermute | solution.py:463
  20.6 20.8 %collective-permute-start.4 = (bf16[208,1024]{1,0:T(8,128)(2,1)}, bf16[208,1024]{1,0:T(8,128)(2,1)S(1)}, u32[]{:S(2)}, u32[]{:S(2)}) collective-permute-start(bf16[208,1024]{1,0:T(8,128)(2,1)} %get-tuple-element.51), channel_id=1, source_target_pairs={{0,16},{8,24},{16,0},{24,8},{1,17},{9,25},{17,1},{25,9},{2,18},{10... | collective-permute-start | bytes 1277960 | tf_op jit(solution)/shard_map/ppermute | solution.py:463
  21.4 20.1 %collective-permute-start.5 = (bf16[208,1024]{1,0:T(8,128)(2,1)S(1)}, bf16[208,1024]{1,0:T(8,128)(2,1)}, u32[]{:S(2)}, u32[]{:S(2)}) collective-permute-start(bf16[208,1024]{1,0:T(8,128)(2,1)S(1)} %get-tuple-element.50), channel_id=1, source_target_pairs={{0,8},{8,16},{16,24},{24,0},{1,9},{9,17},{17,25},{25,1},{2,10},{10... | collective-permute-start | bytes 1277960 | tf_op jit(solution)/shard_map/ppermute | solution.py:463
  41.4 0.8 copy-start.6
  45.6 6.2 %copy-start.1 = (bf16[2,208,1024]{2,1,0:T(8,128)(2,1)S(1)}, bf16[2,208,1024]{2,1,0:T(8,128)(2,1)}, u32[]{:S(2)}) copy-start(bf16[2,208,1024]{2,1,0:T(8,128)(2,1)} %param.11) | copy-start | bytes 2555908
  45.6 30.0 %all-to-all-start.2 = ((bf16[8,2,208,128]{3,2,1,0:T(8,128)(2,1)}), bf16[8,2,208,128]{3,2,1,0:T(8,128)(2,1)S(1)}, u32[]{:S(2)}, u32[]{:S(2)}) async-start(bf16[8,2,208,128]{3,2,1,0:T(8,128)(2,1)} %bitcast.167), calls=%async_computation.2 | async-start | bytes 1703936 | tf_op jit(solution)/shard_map/all_to_all | solution.py:514
  51.9 10.3 %collective-permute-start = (bf16[208,1024]{1,0:T(8,128)(2,1)S(1)}, bf16[208,1024]{1,0:T(8,128)(2,1)S(1)}, u32[]{:S(2)}, u32[]{:S(2)}) collective-permute-start(bf16[208,1024]{1,0:T(8,128)(2,1)S(1)} %get-tuple-element.55), channel_id=1, source_target_pairs={{0,24},{8,0},{16,8},{24,16},{1,25},{9,1},{17,9},{25,17},{2,26},{10... | collective-permute-start | bytes 1277960 | tf_op jit(solution)/shard_map/ppermute | solution.py:463
  51.9 19.2 %collective-permute-start.1 = (bf16[208,1024]{1,0:T(8,128)(2,1)S(1)}, bf16[208,1024]{1,0:T(8,128)(2,1)S(1)}, u32[]{:S(2)}, u32[]{:S(2)}) collective-permute-start(bf16[208,1024]{1,0:T(8,128)(2,1)S(1)} %get-tuple-element.54), channel_id=1, source_target_pairs={{0,16},{8,24},{16,0},{24,8},{1,17},{9,25},{17,1},{25,9},{2,18},{10... | collective-permute-start | bytes 1277960 | tf_op jit(solution)/shard_map/ppermute | solution.py:463
  52.3 19.7 %collective-permute-start.2 = (bf16[208,1024]{1,0:T(8,128)(2,1)S(1)}, bf16[208,1024]{1,0:T(8,128)(2,1)S(1)}, u32[]{:S(2)}, u32[]{:S(2)}) collective-permute-start(bf16[208,1024]{1,0:T(8,128)(2,1)S(1)} %get-tuple-element.53), channel_id=1, source_target_pairs={{0,8},{8,16},{16,24},{24,0},{1,9},{9,17},{17,25},{25,1},{2,10},{10... | collective-permute-start | bytes 1277960 | tf_op jit(solution)/shard_map/ppermute | solution.py:463
  75.6 6.1 %copy-start.8 = (s32[4]{0:T(128)S(1)}, s32[4]{0:T(128)}, u32[]{:S(2)}) copy-start(s32[4]{0:T(128)} %param.16) | copy-start | bytes 52
  75.6 27.0 %all-to-all-start.1 = ((bf16[8,2,208,128]{3,2,1,0:T(8,128)(2,1)}), bf16[8,2,208,128]{3,2,1,0:T(8,128)(2,1)S(1)}, u32[]{:S(2)}, u32[]{:S(2)}) async-start(bf16[8,2,208,128]{3,2,1,0:T(8,128)(2,1)} %bitcast.24), calls=%async_computation.1 | async-start | bytes 1703936 | tf_op jit(solution)/shard_map/all_to_all | solution.py:514
  126.9 3.7 %copy-start.2 = (bf16[2,1664,128]{2,1,0:T(8,128)(2,1)S(1)}, bf16[2,1664,128]{2,1,0:T(8,128)(2,1)}, u32[]{:S(2)}) copy-start(bf16[2,1664,128]{2,1,0:T(8,128)(2,1)} %get-tuple-element.21) | copy-start | bytes 2555908
  126.9 23.7 %all-to-all-start.3 = ((bf16[8,2,208,128]{3,2,1,0:T(8,128)(2,1)}), bf16[8,2,208,128]{3,2,1,0:T(8,128)(2,1)S(1)}, u32[]{:S(2)}, u32[]{:S(2)}) async-start(bf16[8,2,208,128]{3,2,1,0:T(8,128)(2,1)} %bitcast.160), calls=%async_computation.3 | async-start | bytes 1703936 | tf_op jit(solution)/shard_map/all_to_all | solution.py:543
  150.6 40.1 %all-to-all-start.5 = ((bf16[8,2,208,128]{3,2,1,0:T(8,128)(2,1)}), bf16[8,2,208,128]{3,2,1,0:T(8,128)(2,1)S(1)}, u32[]{:S(2)}, u32[]{:S(2)}) async-start(bf16[8,2,208,128]{3,2,1,0:T(8,128)(2,1)} %bitcast.158), calls=%async_computation.5 | async-start | bytes 1703936 | tf_op jit(solution)/shard_map/all_to_all | solution.py:543
  162.6 11.1 %copy-start.4 = (bf16[512,512]{1,0:T(8,128)(2,1)S(1)}, bf16[512,512]{1,0:T(8,128)(2,1)}, u32[]{:S(2)}) copy-start(bf16[512,512]{1,0:T(8,128)(2,1)} %get-tuple-element.14) | copy-start | bytes 1572868
  162.6 11.1 %copy-start.5 = (bf16[512,512]{1,0:T(8,128)(2,1)S(1)}, bf16[512,512]{1,0:T(8,128)(2,1)}, u32[]{:S(2)}) copy-start(bf16[512,512]{1,0:T(8,128)(2,1)} %get-tuple-element.15) | copy-start | bytes 1572868
  163.7 10.1 %collective-permute-start.6 = (bf16[208,1024]{1,0:T(8,128)(2,1)}, bf16[208,1024]{1,0:T(8,128)(2,1)S(1)}, u32[]{:S(2)}, u32[]{:S(2)}) collective-permute-start(bf16[208,1024]{1,0:T(8,128)(2,1)} %get-tuple-element.49), channel_id=1, source_target_pairs={{0,24},{8,0},{16,8},{24,16},{1,25},{9,1},{17,9},{25,17},{2,26},{10... | collective-permute-start | bytes 1277960 | tf_op jit(solution)/shard_map/ppermute | solution.py:463
  163.7 22.3 %collective-permute-start.7 = (bf16[208,1024]{1,0:T(8,128)(2,1)}, bf16[208,1024]{1,0:T(8,128)(2,1)}, u32[]{:S(2)}, u32[]{:S(2)}) collective-permute-start(bf16[208,1024]{1,0:T(8,128)(2,1)} %get-tuple-element.48), channel_id=1, source_target_pairs={{0,16},{8,24},{16,0},{24,8},{1,17},{9,25},{17,1},{25,9},{2,18},{10... | collective-permute-start | bytes 1277960 | tf_op jit(solution)/shard_map/ppermute | solution.py:463
  166.5 19.5 %collective-permute-start.8 = (bf16[208,1024]{1,0:T(8,128)(2,1)}, bf16[208,1024]{1,0:T(8,128)(2,1)}, u32[]{:S(2)}, u32[]{:S(2)}) collective-permute-start(bf16[208,1024]{1,0:T(8,128)(2,1)} %get-tuple-element.47), channel_id=1, source_target_pairs={{0,8},{8,16},{16,24},{24,0},{1,9},{9,17},{17,25},{25,1},{2,10},{10... | collective-permute-start | bytes 1277960 | tf_op jit(solution)/shard_map/ppermute | solution.py:463
  190.7 28.4 %all-to-all-start.4 = ((bf16[2,4,128,512]{3,2,0,1:T(8,128)(2,1)}), bf16[2,4,128,512]{3,2,0,1:T(8,128)(2,1)S(1)}, u32[]{:S(2)}, u32[]{:S(2)}) async-start(bf16[2,4,128,512]{3,2,0,1:T(8,128)(2,1)} %copy.75), calls=%async_computation.4 | async-start | bytes 2097152 | tf_op jit(solution)/shard_map/all_to_all | solution.py:565
  196.8 12.8 %collective-permute-start.10 = (bf16[208,1024]{1,0:T(8,128)(2,1)S(1)}, bf16[208,1024]{1,0:T(8,128)(2,1)S(1)}, u32[]{:S(2)}, u32[]{:S(2)}) collective-permute-start(bf16[208,1024]{1,0:T(8,128)(2,1)S(1)} %get-tuple-element.45), channel_id=1, source_target_pairs={{0,16},{8,24},{16,0},{24,8},{1,17},{9,25},{17,1},{25,9},{2,18},{10... | collective-permute-start | bytes 1277960 | tf_op jit(solution)/shard_map/ppermute | solution.py:463
  197.0 14.7 %collective-permute-start.11 = (bf16[208,1024]{1,0:T(8,128)(2,1)S(1)}, bf16[208,1024]{1,0:T(8,128)(2,1)S(1)}, u32[]{:S(2)}, u32[]{:S(2)}) collective-permute-start(bf16[208,1024]{1,0:T(8,128)(2,1)S(1)} %get-tuple-element.44), channel_id=1, source_target_pairs={{0,8},{8,16},{16,24},{24,0},{1,9},{9,17},{17,25},{25,1},{2,10},{10... | collective-permute-start | bytes 1277960 | tf_op jit(solution)/shard_map/ppermute | solution.py:463
  197.0 17.0 %collective-permute-start.9 = (bf16[208,1024]{1,0:T(8,128)(2,1)S(1)}, bf16[208,1024]{1,0:T(8,128)(2,1)S(1)}, u32[]{:S(2)}, u32[]{:S(2)}) collective-permute-start(bf16[208,1024]{1,0:T(8,128)(2,1)S(1)} %get-tuple-element.46), channel_id=1, source_target_pairs={{0,24},{8,0},{16,8},{24,16},{1,25},{9,1},{17,9},{25,17},{2,26},{10... | collective-permute-start | bytes 1277960 | tf_op jit(solution)/shard_map/ppermute | solution.py:463
